TPU v7x, 32 devices: a whole 2x2x4 slice. The times are simulated.
32 devices in a mesh: dev: 32 (over z, y, x, core).
Axes of the slice: x: 2, y: 2, z: 4, core: 2. Of those that a mesh axis runs over, the one named last changes fastest.
Arguments:
- runs_field: float32 [512, 256, 256], P('dev'), may hold values from -6 to 6
- spectral_filter: float32 [256, 129], replicated, may hold values from 0.3 to 3, as said below
- block_inverses: float32 [2, 256, 256], replicated, may hold values from -1.5 to 1.5, as said below
- factor_panels: float32 [2, 512, 256], P(None, 'dev'), may hold values from -0.375 to 0.375
Outputs:
- solved: float32 [512, 65536], P(None, 'dev')
Inputs may be any that keep to these rules, and one draw needn't show every extreme that they name: `spectral_filter`: symmetric under the first frequency index k -> (256 - k) mod 256 in columns 0 and 128. `block_inverses`: each block is lower triangular with diagonal entries from 0.7 to 1.4.
All inputs are finite; a program needn't handle non-finite values.
Results may differ from a plain program's by a relative error of at most 0.000076.
Values sent between devices are 32-bit elements; how exact they have to be, the bound alone decides.
No kernel may reach another device: no remote copies, remote signals or barrier semaphores. Data moves between devices by JAX's collectives and lax.ppermute only.
A program may use at most 64 MiB of HBM per device.

v0:
```python
import functools, math
LANES = 128
import numpy as np
import jax, jax.numpy as jnp
from jax import lax
from jax.experimental import pallas as pl
from jax.experimental.pallas import tpu as pltpu
from jax.sharding import PartitionSpec as P


def basis(length):
    half, quarter = length // 2, length // 4
    slot = np.arange(half)
    tables = []
    for freq, cosine in (
        (np.where(slot <= quarter, 2 * slot, 2 * slot - half), slot <= quarter),
        (2 * (slot % quarter) + 1, slot < quarter),
    ):
        angle = (np.outer(np.arange(half), freq) % length) * (2.0 * math.pi / length)
        table = np.where(cosine[None, :], np.cos(angle), np.sin(angle))
        hi = table.astype(jnp.bfloat16)
        lo = (table - hi.astype(np.float64)).astype(jnp.bfloat16)
        ahead = np.block([[hi, lo], [hi, lo]])
        back = np.block([[hi.T, lo.T], [hi.T, lo.T]])
        tables += [ahead, ahead.T, back, back.T]
    return tables


def split(x):
    hi = x.astype(jnp.bfloat16)
    lo = (x - hi.astype(jnp.float32)).astype(jnp.bfloat16)
    return hi, lo


def mm(a, b):
    return lax.dot_general(a, b, (((1,), (0,)), ((), ())), preferred_element_type=jnp.float32)


def exact_pick(sel, table, dims):
    out, rest = None, table
    for _ in range(3):
        piece = rest.astype(jnp.bfloat16)
        rest = rest - piece.astype(jnp.float32)
        part = lax.dot_general(sel, piece, (dims, ((), ())), preferred_element_type=jnp.float32)
        out = part if out is None else out + part
    return out


def frequency(slot, length):
    half, quarter = length // 2, length // 4
    within = slot & (half - 1)
    even = jnp.where(within <= quarter, 2 * within, 2 * within - half)
    odd = 2 * (slot & (quarter - 1)) + 1
    return jnp.where(slot < half, even, odd), within < quarter


def gains(filter_t, length):
    half = length // 2
    row = lax.broadcasted_iota(jnp.int32, (length, length), 0)
    col = lax.broadcasted_iota(jnp.int32, (length, length), 1)
    freq, kind = frequency(row, length)
    edge = (freq == 0) | (freq == half)
    plus = (col == freq).astype(jnp.float32)
    minus = jnp.where(edge, 0.0, (col == length - freq).astype(jnp.float32))
    sums = (plus + minus).astype(jnp.bfloat16)
    diffs = (jnp.where(edge, 0.0, plus) - minus).astype(jnp.bfloat16)
    table = exact_pick(plus[:, :half].astype(jnp.bfloat16), filter_t[:half], ((1,), (0,)))
    table = jnp.where(freq == half, jnp.broadcast_to(filter_t[half:half + 1], table.shape), table)
    s = exact_pick(sums, table, ((1,), (1,)))
    d = exact_pick(diffs, table, ((1,), (1,)))
    across, other = frequency(col, length)
    border = (across == 0) | (across == half)
    scale = 1.0 / float(length * length)
    s = s * jnp.where(border, scale, 2.0 * scale)
    d = d * jnp.where(border, 0.0, jnp.where(kind == other, -2.0 * scale, 2.0 * scale))
    return s, d


def whiten_kernel(me_ref, x_ref, ft_ref, *rest, rb, groups, outs):
    tables, rest = rest[:8], rest[8:]
    o_refs, (g1_ref, g2_ref), stage = rest[:outs], rest[outs:outs + 2], rest[outs + 2:]
    length = x_ref.shape[1]
    half, quarter = length // 2, length // 4

    @pl.when(pl.program_id(0) == 0)
    def _():
        s, d = gains(ft_ref[...], length)
        g1_ref[...] = s
        g2_ref[...] = d

    even, even_t, even_back, even_back_t, odd, odd_t, odd_back, odd_back_t = (ref[...] for ref in tables)

    def right(x, table):
        out = mm(jnp.concatenate(split(x), axis=1), table)
        return out[:, :half] + out[:, half:]

    def left(table, x):
        out = mm(table, jnp.concatenate(split(x), axis=0))
        return out[:half] + out[half:]

    x = x_ref[...].reshape(rb * length, length)
    x0, x1 = x[:, :half], x[:, half:]
    z = jnp.concatenate([right(x0 + x1, even), right(x0 - x1, odd)], axis=1)
    vs = []
    for r in range(rb):
        z0, z1 = z[r * length:r * length + half], z[r * length + half:(r + 1) * length]
        t = jnp.concatenate([left(even_t, z0 + z1), left(odd_t, z0 - z1)], axis=0)
        sw = jnp.concatenate([t[q * quarter:(q + 1) * quarter] for q in (1, 0, 3, 2)], axis=0)
        sw = jnp.concatenate([pltpu.roll(sw[:, :half], quarter, 1), pltpu.roll(sw[:, half:], quarter, 1)], axis=1)
        t = g1_ref[...] * t + g2_ref[...] * sw
        e, o = left(even_back_t, t[:half]), left(odd_back_t, t[half:])
        vs += [e + o, e - o]
    v = jnp.concatenate(vs, axis=0)
    e, o = right(v[:, :half], even_back), right(v[:, half:], odd_back)
    y = jnp.concatenate([e + o, e - o], axis=1)
    rows = length // groups
    target = stage[0] if stage else o_refs[0]
    for r in range(rb):
        for part in range(length // LANES):
            target[:, r, part] = y[r * length:(r + 1) * length, part * LANES:(part + 1) * LANES].reshape(groups, rows, LANES)
    if stage:
        chip = me_ref[0] // 2
        for k, o_ref in enumerate(o_refs[:groups // 4]):
            o_ref[...] = target[pl.ds(2 * (chip ^ k), 2)]
        for way, o_ref in enumerate(o_refs[groups // 4:], groups // 2):
            o_ref[...] = target[pl.ds(me_ref[0] ^ way, 1)]


def whiten(me, x, spectral_filter, groups, start, count, rb, spread):
    length = x.shape[1]
    rows, parts = length // groups, length // LANES
    tables = basis(length)
    const = lambda shape: pl.BlockSpec(shape, lambda i, me: (0,) * len(shape), pipeline_mode=pl.Buffered(1))
    off = start // rb
    leads = [2] * (groups // 4) + [1] * (groups // 2) if spread else [groups]
    scratch = [pltpu.VMEM((length, length), jnp.float32)] * 2
    if spread:
        scratch.append(pltpu.VMEM((groups, rb, parts, rows, LANES), jnp.float32))
    return pl.pallas_call(
        functools.partial(whiten_kernel, rb=rb, groups=groups, outs=len(leads)),
        grid_spec=pltpu.PrefetchScalarGridSpec(
            num_scalar_prefetch=1,
            grid=(count // rb,),
            in_specs=[pl.BlockSpec((rb, length, length), lambda i, me: (i + off, 0, 0)),
                      const((spectral_filter.shape[1], length))] + [const((length, length))] * 8,
            out_specs=[pl.BlockSpec((lead, rb, parts, rows, LANES), lambda i, me: (0, i, 0, 0, 0)) for lead in leads],
            scratch_shapes=scratch,
        ),
        out_shape=[jax.ShapeDtypeStruct((lead, count, parts, rows, LANES), jnp.float32) for lead in leads],
        name="whiten",
    )(me, x, spectral_filter.T, *tables)


def plain_kernel(w_ref, mh_ref, ml_ref, o_ref, *, rows, parts):
    k = mh_ref.shape[1]
    i = pl.program_id(0)
    w = jnp.concatenate([w_ref[pl.ds(p * rows + i, k, stride=rows * parts), :] for p in range(parts)], axis=1)
    wh, wl = split(w)
    o_ref[...] = mm(mh_ref[...], wh) + mm(mh_ref[...], wl) + mm(ml_ref[...], wh)


def plain_solve(w, mh, ml, rows, parts):
    q = mh.shape[0]
    const = lambda a: pl.BlockSpec(a.shape, lambda i: (0,) * a.ndim, pipeline_mode=pl.Buffered(1))
    return pl.pallas_call(
        functools.partial(plain_kernel, rows=rows, parts=parts),
        grid=(rows,),
        in_specs=[const(w), const(mh), const(ml)],
        out_specs=pl.BlockSpec((q, parts * LANES), lambda i: (0, i)),
        out_shape=jax.ShapeDtypeStruct((q, rows * parts * LANES), jnp.float32),
        name="plain",
    )(w, mh, ml)


def whole(shape):
    return pl.BlockSpec(shape, lambda i, me: (0,) * len(shape), pipeline_mode=pl.Buffered(1))


def outside(arrays):
    return [pltpu.with_memory_space_constraint(a, pltpu.HBM) for a in arrays]


def parity(array, flip):
    pick = (lambda i, me: (1 - me[0] % 2, 0, 0)) if flip else (lambda i, me: (me[0] % 2, 0, 0))
    return pl.BlockSpec((None,) + array.shape[1:], pick, pipeline_mode=pl.Buffered(1))


def bundle_kernel(me_ref, *refs):
    size = refs[0].shape[0]
    for j, ref in enumerate(refs[:-1]):
        refs[-1][j * size:(j + 1) * size] = ref[...]


def bundle(me, arrays):
    size = arrays[0].shape[1]
    shape = (len(arrays) * size, LANES)
    return pl.pallas_call(
        bundle_kernel,
        grid_spec=pltpu.PrefetchScalarGridSpec(
            num_scalar_prefetch=1, grid=(1,), in_specs=[parity(a, True) for a in arrays], out_specs=whole(shape)),
        out_shape=jax.ShapeDtypeStruct(shape, jnp.float32),
        name="bundle",
    )(me, *arrays)


def stack(me, arrays):
    rows, lanes = arrays[0].shape
    shape = (len(arrays) * rows, lanes)
    return pl.pallas_call(
        bundle_kernel,
        grid_spec=pltpu.PrefetchScalarGridSpec(
            num_scalar_prefetch=1, grid=(1,), in_specs=[whole(a.shape) for a in arrays], out_specs=whole(shape)),
        out_shape=jax.ShapeDtypeStruct(shape, jnp.float32),
        name="stack",
    )(me, *arrays)


def mix_kernel(me_ref, *refs, top, local, stages):
    orders, (inverse_ref, *papers, theirs_ref) = refs[:2 * stages], refs[2 * stages:-2 * stages - 1]
    o_refs, panel_ref = refs[-2 * stages - 1:-1], refs[-1]
    me = me_ref[0]
    for k, ref in enumerate(papers):
        for c in range(2):
            at = pl.multiple_of(((me ^ (2 * k + c)) & (top - 1)) * local, local)
            panel_ref[pl.ds(at, local), :] = theirs_ref[k * local:(k + 1) * local] if c else ref[...]
    exact = functools.partial(jnp.dot, precision=lax.Precision.HIGHEST, preferred_element_type=jnp.float32)
    first, second = inverse_ref[0], inverse_ref[1]
    below = -exact(second, exact(panel_ref[...], first))
    table = jnp.concatenate([
        jnp.concatenate([first, jnp.zeros_like(first)], axis=1),
        jnp.concatenate([below, second], axis=1)], axis=0)
    pieces = split(table)
    for n in range(stages):
        spot_ref, mask_ref = orders[2 * n:2 * n + 2]
        run = spot_ref[...] ^ ((me * local) & mask_ref[...])
        shape = (table.shape[0], run.shape[1])
        order = lax.broadcasted_iota(jnp.int32, shape, 0) == jnp.broadcast_to(run, shape)
        order = order.astype(jnp.float32).astype(jnp.bfloat16)
        for piece, o_ref in zip(pieces, o_refs[2 * n:2 * n + 2]):
            o_ref[...] = mm(piece, order).astype(jnp.bfloat16)


def mix(me, orders, inverses, papers, theirs, top, local):
    width = inverses.shape[1]
    flat = [table for order in orders for table in order]
    args = [*flat, inverses, *papers, theirs]
    shapes = [(2 * width, table.shape[1]) for table in flat]
    return pl.pallas_call(
        functools.partial(mix_kernel, top=top, local=local, stages=len(orders)),
        grid_spec=pltpu.PrefetchScalarGridSpec(
            num_scalar_prefetch=1, grid=(1,),
            in_specs=[whole(a.shape) for a in args],
            out_specs=[whole(shape) for shape in shapes],
            scratch_shapes=[pltpu.VMEM((width, width), jnp.float32)]),
        out_shape=[jax.ShapeDtypeStruct(shape, jnp.bfloat16) for shape in shapes],
        name="mix",
    )(me, *args)


def solve_kernel(me_ref, *refs, rows, parts, per, sizes, acc):
    n = len(sizes)
    mh_ref, ml_ref = refs[n:n + 2]
    o_ref = refs[-1]
    columns = []
    for g in range(per):
        i = pl.program_id(0) * per + g
        for p in range(parts):
            column = [ref[pl.ds(p * rows + i, k, stride=rows * parts), :] for ref, k in zip(refs, sizes)]
            columns.append(jnp.concatenate(column, axis=0))
    wh, wl = split(jnp.concatenate(columns, axis=1))
    mh, ml = mh_ref[...], ml_ref[...]
    out = mm(mh, wh) + mm(mh, wl) + mm(ml, wh)
    o_ref[...] = out + refs[n + 2][...] if acc else out


def solve(me, pieces, tables, rows, parts, acc=None):
    each = rows * parts
    per = max(d for d in (4, 2, 1) if rows % d == 0)
    width = tables[0].shape[0]
    sizes = [a.shape[-2] // each for a in pieces]
    args = [*pieces, *outside(tables)]
    specs = [parity(a, False) if a.ndim == 3 else whole(a.shape) for a in args]
    tile = pl.BlockSpec((width, per * parts * LANES), lambda i, me: (0, i))
    if acc is not None:
        args.append(acc)
        specs.append(tile)
    return pl.pallas_call(
        functools.partial(solve_kernel, rows=rows, parts=parts, per=per, sizes=tuple(sizes), acc=acc is not None),
        grid_spec=pltpu.PrefetchScalarGridSpec(
            num_scalar_prefetch=1, grid=(rows // per,), in_specs=specs, out_specs=tile),
        out_shape=jax.ShapeDtypeStruct((width, each * LANES), jnp.float32),
        input_output_aliases={} if acc is None else {len(args): 0},
        compiler_params=None if acc is None else pltpu.CompilerParams(vmem_limit_bytes=24 << 20),
        name="solve",
    )(me, *args)


def finish_kernel(me_ref, *refs, rows, parts, sizes):
    n = len(sizes)
    mh_ref, ml_ref, acc_ref, o_ref, held_ref, in_sems, out_sems = refs[n:]
    span = parts * LANES
    mh, ml = mh_ref[...], ml_ref[...]

    def tile(ref, i):
        return ref.at[:, i * span:(i + 1) * span]

    def fetch(i):
        return pltpu.make_async_copy(tile(acc_ref, i), held_ref.at[i], in_sems.at[i])

    def store(i):
        return pltpu.make_async_copy(held_ref.at[i], tile(o_ref, i), out_sems.at[i])

    for i in range(rows):
        fetch(i).start()
    for i in range(rows):
        columns = []
        for p in range(parts):
            column = [ref[pl.ds(p * rows + i, k, stride=rows * parts), :] for ref, k in zip(refs, sizes)]
            columns.append(jnp.concatenate(column, axis=0))
        wh, wl = split(jnp.concatenate(columns, axis=1))
        out = mm(mh, wh) + mm(mh, wl) + mm(ml, wh)
        fetch(i).wait()
        held_ref[i] = held_ref[i] + out
        store(i).start()
    for i in range(rows):
        store(i).wait()


def finish(me, pieces, tables, rows, parts, acc):
    each = rows * parts
    width = tables[0].shape[0]
    sizes = [a.shape[-2] // each for a in pieces]
    args = [*pieces, *outside(tables)]
    specs = [parity(a, False) if a.ndim == 3 else whole(a.shape) for a in args]
    return pl.pallas_call(
        functools.partial(finish_kernel, rows=rows, parts=parts, sizes=tuple(sizes)),
        grid_spec=pltpu.PrefetchScalarGridSpec(
            num_scalar_prefetch=1, grid=(1,), in_specs=[*specs, pl.BlockSpec(memory_space=pl.ANY)],
            out_specs=pl.BlockSpec(memory_space=pl.ANY),
            scratch_shapes=[pltpu.VMEM((rows, width, parts * LANES), jnp.float32),
                            pltpu.SemaphoreType.DMA((rows,)), pltpu.SemaphoreType.DMA((rows,))]),
        out_shape=jax.ShapeDtypeStruct((width, each * LANES), jnp.float32),
        input_output_aliases={len(args) + 1: 0},
        compiler_params=pltpu.CompilerParams(vmem_limit_bytes=24 << 20),
        name="finish",
    )(me, *args, acc)


def precise_dot(a, b):
    return jnp.dot(a, b, precision=lax.Precision.HIGHEST, preferred_element_type=jnp.float32)


def split_outside(x):
    hi = lax.reduce_precision(x, 8, 7)
    return hi.astype(jnp.bfloat16), (x - hi).astype(jnp.bfloat16)


def mixing(block_inverses, panels, total):
    width = block_inverses.shape[1]
    first, second = block_inverses[0], block_inverses[1]
    below = -precise_dot(second, precise_dot(panels[0, width : 2 * width], first))
    top = jnp.concatenate([first, jnp.zeros_like(first)], axis=1)
    rows = [top, jnp.concatenate([below, second], axis=1)]
    if total > 2 * width:
        left, right = panels[0, 2 * width :], panels[1, 2 * width :]
        rows.append(
            -jnp.concatenate(
                [precise_dot(left, first) + precise_dot(right, below), precise_dot(right, second)],
                axis=1,
            )
        )
    return jnp.concatenate(rows, axis=0)


HEAD = 4
SOON = 6
NEAR_SOON = 5


def exchange(x, offset):
    pairs = [(i, i ^ offset) for i in range(lax.axis_size("dev"))]
    return lax.ppermute(x, "dev", pairs)


def general(me, runs_field, spectral_filter, block_inverses, factor_panels):
    groups = lax.axis_size("dev")
    local, length, _ = runs_field.shape
    total = local * groups
    front = 2 * block_inverses.shape[1]
    rows, parts = length // groups, length // LANES
    (pieces,) = whiten(me, runs_field, spectral_filter, groups, 0, local, HEAD, False)
    runs = lax.all_to_all(pieces, "dev", 0, 0, tiled=True).reshape(total, parts, rows, LANES)
    panels = lax.all_gather(factor_panels, "dev", axis=1, tiled=True)
    tables = split_outside(mixing(block_inverses, panels, total))
    out = plain_solve(runs[:front].reshape(-1, LANES), *tables, rows, parts)
    if total > front:
        below = jnp.moveaxis(runs[front:], 1, 2).reshape(total - front, -1)
        out = jnp.concatenate([out[:front], out[front:] + below], axis=0)
    return out


def places(groups, local):
    top = groups // 2
    rest = range(HEAD, local)
    head = [(source * local + r, 0) for source in range(groups) for r in range(HEAD)]
    ways = lambda picks: [(way * local + r, -1) for way in picks for r in rest]
    near, far = list(range(0, top, 2)), list(range(top, groups))
    soon = head + ways(near[:NEAR_SOON]) + ways(far[:SOON])
    last = ways(range(1, top, 2)) + ways(near[NEAR_SOON:]) + ways(far[SOON:])
    return [np.array(stage, np.int32).T.reshape(2, 1, -1) for stage in (soon, last)]


def per_device(runs_field, spectral_filter, block_inverses, factor_panels):
    groups = lax.axis_size("dev")
    place = lax.axis_index("dev")
    local, length, _ = runs_field.shape
    width = block_inverses.shape[1]
    rows, parts = length // groups, length // LANES
    chips, top = groups // 2, groups // 2
    me = place.astype(jnp.int32).reshape(1)
    if local * groups != 2 * width:
        return general(me, runs_field, spectral_filter, block_inverses, factor_panels)
    rest = local - HEAD
    near = list(range(1, chips // 2))
    mine = factor_panels[0]
    mine = jnp.where(place < top, exchange(mine, top), mine)
    (head,) = whiten(me, runs_field, spectral_filter, groups, 0, HEAD, HEAD // 2, False)
    head = lax.all_to_all(head, "dev", 0, 0, tiled=True)
    outs = whiten(me, runs_field, spectral_filter, groups, HEAD, rest, HEAD, True)
    got = [outs[0].reshape(2, -1, LANES)]
    papers = [mine]
    for k in near:
        papers.append(exchange(mine, 2 * k))
    for k in near:
        got.append(exchange(outs[k].reshape(2, -1, LANES), 2 * k))
    direct = []
    for way in range(top, groups):
        direct.append(exchange(outs[way - chips // 2].reshape(-1, LANES), way))
    theirs = exchange(stack(me, papers), 1)
    tables = mix(me, places(groups, local), block_inverses, papers, theirs, top, local)
    load = bundle(me, got)
    load = exchange(load, 1)
    out = solve(me, outside([head.reshape(-1, LANES), *got[:NEAR_SOON], *direct[:SOON]]), tables[:2], rows, parts)
    return finish(me, [load, *outside(got[NEAR_SOON:]), *direct[SOON:]], tables[2:], rows, parts, out)


def solution(mesh):
    return jax.shard_map(
        per_device,
        mesh=mesh,
        in_specs=(P("dev", None, None), P(), P(), P(None, "dev", None)),
        out_specs=P(None, "dev"),
        check_vma=False,
    )
```

profile of v0, /device:TPU:0, one launch (start us, length us, event | category | flops | bytes accessed | tf_op | source)
XLA Modules:
  0.0 147.1 jit_solution(2314522413179531850)
XLA Ops:
  0.0 5.6 %whiten.3 = f32[32,4,2,8,128]{4,3,2,1,0:T(8,128)} custom-call(s32[1]{0:T(128)} %bitcast.me_ref, f32[16,256,256]{2,1,0:T(8,128)} %x_ref.3, f32[129,256]{1,0:T(8,128)} %bitcast.34, bf16[256,256]{1,0:T(8,128)(2,1)} %constant.30.clone.rest_0_, bf16[256,256]{1,0:T(8,128)(2,1)} %constant.31.clone.rest_1_, bf16[256,256]{1,0:T(8,128)(2,1)} %constant.32.clone.rest_2_, ...), custom_call_target="tpu_custom_call" | custom-call | tf_op jit(solution)/shard_map/whiten/pallas_call | solution.py:139
  5.6 7.3 %all-to-all-start = ((f32[32,4,2,8,128]{4,3,2,1,0:T(8,128)}), f32[32,4,2,8,128]{4,3,2,1,0:T(8,128)S(1)}, u32[]{:S(2)}, u32[]{:S(2)}) async-start(f32[32,4,2,8,128]{4,3,2,1,0:T(8,128)} %whiten.3), calls=%async_computation | async-start | bytes 2097152 | tf_op jit(solution)/shard_map/all_to_all | solution.py:428
  13.0 10.7 %whiten.2 = (f32[2,12,2,8,128]{4,3,2,1,0:T(8,128)}, f32[2,12,2,8,128]{4,3,2,1,0:T(8,128)}, f32[2,12,2,8,128]{4,3,2,1,0:T(8,128)}, f32[2,12,2,8,128]{4,3,2,1,0:T(...) custom-call(s32[1]{0:T(128)} %bitcast.me_ref, ...), custom_call_target="tpu_custom_call" | custom-call | tf_op jit(solution)/shard_map/whiten/pallas_call | solution.py:139
  23.7 1.8 %collective-permute-start = (f32[2,192,128]{2,1,0:T(8,128)}, f32[2,192,128]{2,1,0:T(8,128)S(1)}, u32[]{:S(2)}, u32[]{:S(2)}) collective-permute-start(f32[2,192,128]{2,1,0:T(8,128)} %bitcast.42), channel_id=1, source_target_pairs={{0,2},{1,3},{2,0},{3,1},{4,6},{5,7},{6,4},{7,5},{8,10},{9,11},{10,... | collective-permute-start | bytes 589832 | tf_op jit(solution)/shard_map/ppermute | solution.py:382
  30.5 2.7 %collective-permute-done.refs_1_.refs_2_ = f32[2,192,128]{2,1,0:T(8,128)S(1)} collective-permute-done((f32[2,192,128]{2,1,0:T(8,128)}, f32[2,192,128]{2,1,0:T(8,128)S(1)}, u32[]{:S(2)}, u32[]{:S(2)}) %collective-permute-start) | collective-permute-done | bytes 196640 | tf_op jit(solution)/shard_map/ppermute | solution.py:382
  33.2 3.0 %collective-permute-start.5 = (f32[2,192,128]{2,1,0:T(8,128)}, f32[2,192,128]{2,1,0:T(8,128)S(1)}, u32[]{:S(2)}, u32[]{:S(2)}) collective-permute-start(f32[2,192,128]{2,1,0:T(8,128)} %bitcast.37), channel_id=1, source_target_pairs={{0,12},{1,13},{2,14},{3,15},{4,8},{5,9},{6,10},{7,11},{8,4},{9,5},... | collective-permute-start | bytes 589832 | tf_op jit(solution)/shard_map/ppermute | solution.py:382
  36.2 2.8 %collective-permute-done.1.refs_2_.refs_3_ = f32[2,192,128]{2,1,0:T(8,128)S(1)} collective-permute-done((f32[2,192,128]{2,1,0:T(8,128)}, f32[2,192,128]{2,1,0:T(8,128)S(1)}, u32[]{:S(2)}, u32[]{:S(2)}) %collective-permute-start.1) | collective-permute-done | bytes 196640 | tf_op jit(solution)/shard_map/ppermute | solution.py:382
  40.2 4.4 %collective-permute-done.4.refs_5_.refs_1_ = f32[2,192,128]{2,1,0:T(8,128)S(1)} collective-permute-done((f32[2,192,128]{2,1,0:T(8,128)}, f32[2,192,128]{2,1,0:T(8,128)S(1)}, u32[]{:S(2)}, u32[]{:S(2)}) %collective-permute-start.4) | collective-permute-done | bytes 196640 | tf_op jit(solution)/shard_map/ppermute | solution.py:382
  44.6 4.1 %collective-permute-done.5.refs_6_.refs_2_ = f32[2,192,128]{2,1,0:T(8,128)S(1)} collective-permute-done((f32[2,192,128]{2,1,0:T(8,128)}, f32[2,192,128]{2,1,0:T(8,128)S(1)}, u32[]{:S(2)}, u32[]{:S(2)}) %collective-permute-start.5) | collective-permute-done | bytes 196640 | tf_op jit(solution)/shard_map/ppermute | solution.py:382
  48.7 4.6 %collective-permute-done.6.refs_7_.refs_3_ = f32[2,192,128]{2,1,0:T(8,128)S(1)} collective-permute-done((f32[2,192,128]{2,1,0:T(8,128)}, f32[2,192,128]{2,1,0:T(8,128)S(1)}, u32[]{:S(2)}, u32[]{:S(2)}) %collective-permute-start.6) | collective-permute-done | bytes 196640 | tf_op jit(solution)/shard_map/ppermute | solution.py:382
  54.0 2.2 %bundle.1 = f32[1536,128]{1,0:T(8,128)} custom-call(s32[1]{0:T(128)} %bitcast.me_ref, f32[2,192,128]{2,1,0:T(8,128)} %bitcast.32, f32[2,192,128]{2,1,0:T(8,128)} %copy-done.4, f32[2,192,128]{2,1,0:T(8,128)} %copy-done.5, f32[2,192,128]{2,1,0:T(8,128)} %copy-done.6, f32[2,192,128]{2,1,0:T(8,128)} %copy-done.7, f32[2,192,128]{2,1,0:T(8,128)} %copy-done.1, ...), custom_call_target="tpu_custom_call" | custom-call | tf_op jit(solution)/shard_map/bundle/pallas_call | solution.py:197
  56.2 1.9 %collective-permute-start.18 = (f32[16,256]{1,0:T(8,128)S(1)}, f32[16,256]{1,0:T(8,128)S(1)}, u32[]{:S(2)}, u32[]{:S(2)}) collective-permute-start(f32[16,256]{1,0:T(8,128)S(1)} %slice_bitcast_fusion), channel_id=1, source_target_pairs={{0,16},{1,17},{2,18},{3,19},{4,20},{5,21},{6,22},{7,23},{8,24},{9,... | collective-permute-start | bytes 49160 | tf_op jit(solution)/shard_map/ppermute | solution.py:382
  58.8 2.3 %collective-permute-done.18 = f32[16,256]{1,0:T(8,128)S(1)} collective-permute-done((f32[16,256]{1,0:T(8,128)S(1)}, f32[16,256]{1,0:T(8,128)S(1)}, u32[]{:S(2)}, u32[]{:S(2)}) %collective-permute-start.18) | collective-permute-done | bytes 16416 | tf_op jit(solution)/shard_map/ppermute | solution.py:382
  62.1 1.9 %collective-permute-start.24 = (f32[16,256]{1,0:T(8,128)S(1)}, f32[16,256]{1,0:T(8,128)S(1)}, u32[]{:S(2)}, u32[]{:S(2)}) collective-permute-start(f32[16,256]{1,0:T(8,128)S(1)} %broadcast_select_fusion.refs_0_.refs_5_), channel_id=1, source_target_pairs={{0,12},{1,13},{2,14},{3,15},{4,8},{5,9},{6,10},{7,11},{8,4},{9,5},... | collective-permute-start | bytes 49160 | tf_op jit(solution)/shard_map/ppermute | solution.py:382
  65.3 3.0 %collective-permute-done.25.refs_7_.refs_12_ = f32[16,256]{1,0:T(8,128)S(1)} collective-permute-done((f32[16,256]{1,0:T(8,128)S(1)}, f32[16,256]{1,0:T(8,128)S(1)}, u32[]{:S(2)}, u32[]{:S(2)}) %collective-permute-start.25) | collective-permute-done | bytes 16416 | tf_op jit(solution)/shard_map/ppermute | solution.py:382
  69.1 2.9 %collective-permute-done.22.refs_4_.refs_9_ = f32[16,256]{1,0:T(8,128)S(1)} collective-permute-done((f32[16,256]{1,0:T(8,128)S(1)}, f32[16,256]{1,0:T(8,128)S(1)}, u32[]{:S(2)}, u32[]{:S(2)}) %collective-permute-start.22) | collective-permute-done | bytes 16416 | tf_op jit(solution)/shard_map/ppermute | solution.py:382
  73.8 2.4 %collective-permute-done.20.refs_2_.refs_7_ = f32[16,256]{1,0:T(8,128)S(1)} collective-permute-done((f32[16,256]{1,0:T(8,128)S(1)}, f32[16,256]{1,0:T(8,128)S(1)}, u32[]{:S(2)}, u32[]{:S(2)}) %collective-permute-start.20) | collective-permute-done | bytes 16416 | tf_op jit(solution)/shard_map/ppermute | solution.py:382
  77.0 2.4 %collective-permute-start.11 = (f32[192,128]{1,0:T(8,128)}, f32[192,128]{1,0:T(8,128)S(1)}, u32[]{:S(2)}, u32[]{:S(2)}) collective-permute-start(f32[192,128]{1,0:T(8,128)} %bitcast.55), channel_id=1, source_target_pairs={{0,25},{1,24},{2,27},{3,26},{4,29},{5,28},{6,31},{7,30},{8,17},{9,... | collective-permute-start | bytes 294920 | tf_op jit(solution)/shard_map/ppermute | solution.py:382
  79.4 3.0 %collective-permute-start.12 = (f32[192,128]{1,0:T(8,128)}, f32[192,128]{1,0:T(8,128)S(1)}, u32[]{:S(2)}, u32[]{:S(2)}) collective-permute-start(f32[192,128]{1,0:T(8,128)} %bitcast.54), channel_id=1, source_target_pairs={{0,26},{1,27},{2,24},{3,25},{4,30},{5,31},{6,28},{7,29},{8,18},{9,... | collective-permute-start | bytes 294920 | tf_op jit(solution)/shard_map/ppermute | solution.py:382
  82.4 1.8 %collective-permute-start.13 = (f32[192,128]{1,0:T(8,128)}, f32[192,128]{1,0:T(8,128)S(1)}, u32[]{:S(2)}, u32[]{:S(2)}) collective-permute-start(f32[192,128]{1,0:T(8,128)} %bitcast.53), channel_id=1, source_target_pairs={{0,27},{1,26},{2,25},{3,24},{4,31},{5,30},{6,29},{7,28},{8,19},{9,... | collective-permute-start | bytes 294920 | tf_op jit(solution)/shard_map/ppermute | solution.py:382
  84.2 7.3 %collective-permute-start.27 = (f32[192,128]{1,0:T(8,128)}, f32[192,128]{1,0:T(8,128)S(1)}, u32[]{:S(2)}, u32[]{:S(2)}) collective-permute-start(f32[192,128]{1,0:T(8,128)} %bitcast.52), channel_id=1, source_target_pairs={{0,16},{1,17},{2,18},{3,19},{4,20},{5,21},{6,22},{7,23},{8,24},{9,... | collective-permute-start | bytes 294920 | tf_op jit(solution)/shard_map/ppermute | solution.py:382
  93.0 3.6 %collective-permute-start.29 = (f32[192,128]{1,0:T(8,128)}, f32[192,128]{1,0:T(8,128)S(1)}, u32[]{:S(2)}, u32[]{:S(2)}) collective-permute-start(f32[192,128]{1,0:T(8,128)} %bitcast.50), channel_id=1, source_target_pairs={{0,18},{1,19},{2,16},{3,17},{4,22},{5,23},{6,20},{7,21},{8,26},{9,... | collective-permute-start | bytes 294920 | tf_op jit(solution)/shard_map/ppermute | solution.py:382
  98.2 5.3 %collective-permute-done.27.refs_6_ = f32[192,128]{1,0:T(8,128)S(1)} collective-permute-done((f32[192,128]{1,0:T(8,128)}, f32[192,128]{1,0:T(8,128)S(1)}, u32[]{:S(2)}, u32[]{:S(2)}) %collective-permute-start.27) | collective-permute-done | bytes 98336 | tf_op jit(solution)/shard_map/ppermute | solution.py:382
  103.7 2.5 %collective-permute-done.28.refs_7_ = f32[192,128]{1,0:T(8,128)S(1)} collective-permute-done((f32[192,128]{1,0:T(8,128)}, f32[192,128]{1,0:T(8,128)S(1)}, u32[]{:S(2)}, u32[]{:S(2)}) %collective-permute-start.28) | collective-permute-done | bytes 98336 | tf_op jit(solution)/shard_map/ppermute | solution.py:382
  106.3 7.2 %collective-permute-done.29.refs_8_ = f32[192,128]{1,0:T(8,128)S(1)} collective-permute-done((f32[192,128]{1,0:T(8,128)}, f32[192,128]{1,0:T(8,128)S(1)}, u32[]{:S(2)}, u32[]{:S(2)}) %collective-permute-start.29) | collective-permute-done | bytes 98336 | tf_op jit(solution)/shard_map/ppermute | solution.py:382
  116.3 2.3 %collective-permute-done.31.refs_10_ = f32[192,128]{1,0:T(8,128)S(1)} collective-permute-done((f32[192,128]{1,0:T(8,128)}, f32[192,128]{1,0:T(8,128)S(1)}, u32[]{:S(2)}, u32[]{:S(2)}) %collective-permute-start.31) | collective-permute-done | bytes 98336 | tf_op jit(solution)/shard_map/ppermute | solution.py:382
  118.6 2.5 %collective-permute-start.15 = (f32[192,128]{1,0:T(8,128)}, f32[192,128]{1,0:T(8,128)S(1)}, u32[]{:S(2)}, u32[]{:S(2)}) collective-permute-start(f32[192,128]{1,0:T(8,128)} %bitcast.45), channel_id=1, source_target_pairs={{0,29},{1,28},{2,31},{3,30},{4,25},{5,24},{6,27},{7,26},{8,21},{9,... | collective-permute-start | bytes 294920 | tf_op jit(solution)/shard_map/ppermute | solution.py:382
  121.1 2.5 %collective-permute-start.16 = (f32[192,128]{1,0:T(8,128)}, f32[192,128]{1,0:T(8,128)S(1)}, u32[]{:S(2)}, u32[]{:S(2)}) collective-permute-start(f32[192,128]{1,0:T(8,128)} %bitcast.44), channel_id=1, source_target_pairs={{0,30},{1,31},{2,28},{3,29},{4,26},{5,27},{6,24},{7,25},{8,22},{9,... | collective-permute-start | bytes 294920 | tf_op jit(solution)/shard_map/ppermute | solution.py:382
  123.6 3.2 %collective-permute-start.17 = (f32[192,128]{1,0:T(8,128)}, f32[192,128]{1,0:T(8,128)S(1)}, u32[]{:S(2)}, u32[]{:S(2)}) collective-permute-start(f32[192,128]{1,0:T(8,128)} %bitcast.43), channel_id=1, source_target_pairs={{0,31},{1,30},{2,29},{3,28},{4,27},{5,26},{6,25},{7,24},{8,23},{9,... | collective-permute-start | bytes 294920 | tf_op jit(solution)/shard_map/ppermute | solution.py:382
  127.4 3.9 %mix.1 = (bf16[512,260]{1,0:T(8,128)(2,1)}, bf16[512,260]{1,0:T(8,128)(2,1)}, bf16[512,252]{1,0:T(8,128)(2,1)}, bf16[512,252]{1,0:T(8,128)(2,1)}) custom-call(s32[1]{0:T(128)} %bitcast.me_ref, s32[1,260]{1,0:T(1,128)} %constant.38.clone.refs_0_, s32[1,260]{1,0:T(1,128)} %constant.39.clone.refs_1_, s32[1,252]{1,0:T(1,128)} %constant.40.clone.refs_2_, ...), custom_call_target="tpu_custom_call" | custom-call | tf_op jit(solution)/shard_map/mix/pallas_call | solution.py:248
  132.4 7.1 %solve.1.refs_16_ = f32[512,2048]{1,0:T(8,128)} custom-call(s32[1]{0:T(128)} %bitcast.me_ref, f32[2048,128]{1,0:T(8,128)} %bitcast.31, f32[2,192,128]{2,1,0:T(8,128)} %bitcast.33, f32[2,192,128]{2,1,0:T(8,128)} %copy-done.4, f32[2,192,128]{2,1,0:T(8,128)} %copy-done.5, f32[2,192,128]{2,1,0:T(8,128)} %copy-done.6, f32[2,192,128]{2,1,0:T(8,128)} %copy-done.7, ...), custom_call_target="tpu_custom_call" | custom-call | tf_op jit(solution)/shard_map/solve/pallas_call | solution.py:287
  139.5 7.6 %finish.1 = f32[512,2048]{1,0:T(8,128)} custom-call(s32[1]{0:T(128)} %bitcast.me_ref, f32[1536,128]{1,0:T(8,128)S(1)} %collective-permute-done.7.refs_0_, f32[2,192,128]{2,1,0:T(8,128)} %copy-done.1, f32[2,192,128]{2,1,0:T(8,128)} %copy-done.2, f32[2,192,128]{2,1,0:T(8,128)} %copy-done.3, ...), custom_call_target="tpu_custom_call", output_to_operand_aliasing={{}: (17, {})} | custom-call | tf_op jit(solution)/shard_map/finish/pallas_call | solution.py:335
  (94 shorter events, 21.0 us)
Async XLA Ops:
  5.6 125.7 %all-to-all-start = ((f32[32,4,2,8,128]{4,3,2,1,0:T(8,128)}), f32[32,4,2,8,128]{4,3,2,1,0:T(8,128)S(1)}, u32[]{:S(2)}, u32[]{:S(2)}) async-start(f32[32,4,2,8,128]{4,3,2,1,0:T(8,128)} %whiten.3), calls=%async_computation | async-start | bytes 2097152 | tf_op jit(solution)/shard_map/all_to_all | solution.py:428
  23.7 9.5 %collective-permute-start = (f32[2,192,128]{2,1,0:T(8,128)}, f32[2,192,128]{2,1,0:T(8,128)S(1)}, u32[]{:S(2)}, u32[]{:S(2)}) collective-permute-start(f32[2,192,128]{2,1,0:T(8,128)} %bitcast.42), channel_id=1, source_target_pairs={{0,2},{1,3},{2,0},{3,1},{4,6},{5,7},{6,4},{7,5},{8,10},{9,11},{10,... | collective-permute-start | bytes 589832 | tf_op jit(solution)/shard_map/ppermute | solution.py:382
  25.6 13.5 %collective-permute-start.1 = (f32[2,192,128]{2,1,0:T(8,128)}, f32[2,192,128]{2,1,0:T(8,128)S(1)}, u32[]{:S(2)}, u32[]{:S(2)}) collective-permute-start(f32[2,192,128]{2,1,0:T(8,128)} %bitcast.41), channel_id=1, source_target_pairs={{0,4},{1,5},{2,6},{3,7},{4,0},{5,1},{6,2},{7,3},{8,12},{9,13},{10,... | collective-permute-start | bytes 589832 | tf_op jit(solution)/shard_map/ppermute | solution.py:382
  27.0 13.1 %collective-permute-start.2 = (f32[2,192,128]{2,1,0:T(8,128)}, f32[2,192,128]{2,1,0:T(8,128)S(1)}, u32[]{:S(2)}, u32[]{:S(2)}) collective-permute-start(f32[2,192,128]{2,1,0:T(8,128)} %bitcast.40), channel_id=1, source_target_pairs={{0,6},{1,7},{2,4},{3,5},{4,2},{5,3},{6,0},{7,1},{8,14},{9,15},{10,... | collective-permute-start | bytes 589832 | tf_op jit(solution)/shard_map/ppermute | solution.py:382
  27.3 12.9 %collective-permute-start.3 = (f32[2,192,128]{2,1,0:T(8,128)}, f32[2,192,128]{2,1,0:T(8,128)S(1)}, u32[]{:S(2)}, u32[]{:S(2)}) collective-permute-start(f32[2,192,128]{2,1,0:T(8,128)} %bitcast.39), channel_id=1, source_target_pairs={{0,8},{1,9},{2,10},{3,11},{4,12},{5,13},{6,14},{7,15},{8,0},{9,1},... | collective-permute-start | bytes 589832 | tf_op jit(solution)/shard_map/ppermute | solution.py:382
  29.1 15.5 %collective-permute-start.4 = (f32[2,192,128]{2,1,0:T(8,128)}, f32[2,192,128]{2,1,0:T(8,128)S(1)}, u32[]{:S(2)}, u32[]{:S(2)}) collective-permute-start(f32[2,192,128]{2,1,0:T(8,128)} %bitcast.38), channel_id=1, source_target_pairs={{0,10},{1,11},{2,8},{3,9},{4,14},{5,15},{6,12},{7,13},{8,2},{9,3},... | collective-permute-start | bytes 589832 | tf_op jit(solution)/shard_map/ppermute | solution.py:382
  33.2 15.5 %collective-permute-start.5 = (f32[2,192,128]{2,1,0:T(8,128)}, f32[2,192,128]{2,1,0:T(8,128)S(1)}, u32[]{:S(2)}, u32[]{:S(2)}) collective-permute-start(f32[2,192,128]{2,1,0:T(8,128)} %bitcast.37), channel_id=1, source_target_pairs={{0,12},{1,13},{2,14},{3,15},{4,8},{5,9},{6,10},{7,11},{8,4},{9,5},... | collective-permute-start | bytes 589832 | tf_op jit(solution)/shard_map/ppermute | solution.py:382
  39.1 14.2 %collective-permute-start.6 = (f32[2,192,128]{2,1,0:T(8,128)}, f32[2,192,128]{2,1,0:T(8,128)S(1)}, u32[]{:S(2)}, u32[]{:S(2)}) collective-permute-start(f32[2,192,128]{2,1,0:T(8,128)} %bitcast.36), channel_id=1, source_target_pairs={{0,14},{1,15},{2,12},{3,13},{4,10},{5,11},{6,8},{7,9},{8,6},{9,7},... | collective-permute-start | bytes 589832 | tf_op jit(solution)/shard_map/ppermute | solution.py:382
  56.1 83.4 %collective-permute-start.7 = (f32[1536,128]{1,0:T(8,128)}, f32[1536,128]{1,0:T(8,128)S(1)}, u32[]{:S(2)}, u32[]{:S(2)}) collective-permute-start(f32[1536,128]{1,0:T(8,128)} %bundle.1), channel_id=1, source_target_pairs={{0,1},{1,0},{2,3},{3,2},{4,5},{5,4},{6,7},{7,6},{8,9},{9,8},{10,11... | collective-permute-start | bytes 2359304 | tf_op jit(solution)/shard_map/ppermute | solution.py:382
  56.2 4.9 %collective-permute-start.18 = (f32[16,256]{1,0:T(8,128)S(1)}, f32[16,256]{1,0:T(8,128)S(1)}, u32[]{:S(2)}, u32[]{:S(2)}) collective-permute-start(f32[16,256]{1,0:T(8,128)S(1)} %slice_bitcast_fusion), channel_id=1, source_target_pairs={{0,16},{1,17},{2,18},{3,19},{4,20},{5,21},{6,22},{7,23},{8,24},{9,... | collective-permute-start | bytes 49160 | tf_op jit(solution)/shard_map/ppermute | solution.py:382
  58.0 21.4 %collective-permute-start.8 = (f32[192,128]{1,0:T(8,128)}, f32[192,128]{1,0:T(8,128)S(1)}, u32[]{:S(2)}, u32[]{:S(2)}) collective-permute-start(f32[192,128]{1,0:T(8,128)} %bitcast.58), channel_id=1, source_target_pairs={{0,22},{1,23},{2,20},{3,21},{4,18},{5,19},{6,16},{7,17},{8,30},{9,... | collective-permute-start | bytes 294920 | tf_op jit(solution)/shard_map/ppermute | solution.py:382
  61.0 7.2 %collective-permute-start.25 = (f32[16,256]{1,0:T(8,128)S(1)}, f32[16,256]{1,0:T(8,128)S(1)}, u32[]{:S(2)}, u32[]{:S(2)}) collective-permute-start(f32[16,256]{1,0:T(8,128)S(1)} %broadcast_select_fusion.refs_0_.refs_5_), channel_id=1, source_target_pairs={{0,14},{1,15},{2,12},{3,13},{4,10},{5,11},{6,8},{7,9},{8,6},{9,7},... | collective-permute-start | bytes 49160 | tf_op jit(solution)/shard_map/ppermute | solution.py:382
  62.1 6.2 %collective-permute-start.24 = (f32[16,256]{1,0:T(8,128)S(1)}, f32[16,256]{1,0:T(8,128)S(1)}, u32[]{:S(2)}, u32[]{:S(2)}) collective-permute-start(f32[16,256]{1,0:T(8,128)S(1)} %broadcast_select_fusion.refs_0_.refs_5_), channel_id=1, source_target_pairs={{0,12},{1,13},{2,14},{3,15},{4,8},{5,9},{6,10},{7,11},{8,4},{9,5},... | collective-permute-start | bytes 49160 | tf_op jit(solution)/shard_map/ppermute | solution.py:382
  64.0 5.1 %collective-permute-start.23 = (f32[16,256]{1,0:T(8,128)S(1)}, f32[16,256]{1,0:T(8,128)S(1)}, u32[]{:S(2)}, u32[]{:S(2)}) collective-permute-start(f32[16,256]{1,0:T(8,128)S(1)} %broadcast_select_fusion.refs_0_.refs_5_), channel_id=1, source_target_pairs={{0,10},{1,11},{2,8},{3,9},{4,14},{5,15},{6,12},{7,13},{8,2},{9,3},... | collective-permute-start | bytes 49160 | tf_op jit(solution)/shard_map/ppermute | solution.py:382
  68.3 4.7 %collective-permute-start.21 = (f32[16,256]{1,0:T(8,128)S(1)}, f32[16,256]{1,0:T(8,128)S(1)}, u32[]{:S(2)}, u32[]{:S(2)}) collective-permute-start(f32[16,256]{1,0:T(8,128)S(1)} %broadcast_select_fusion.refs_0_.refs_5_), channel_id=1, source_target_pairs={{0,6},{1,7},{2,4},{3,5},{4,2},{5,3},{6,0},{7,1},{8,14},{9,15},{10,... | collective-permute-start | bytes 49160 | tf_op jit(solution)/shard_map/ppermute | solution.py:382
  69.1 13.3 %collective-permute-start.9 = (f32[192,128]{1,0:T(8,128)}, f32[192,128]{1,0:T(8,128)S(1)}, u32[]{:S(2)}, u32[]{:S(2)}) collective-permute-start(f32[192,128]{1,0:T(8,128)} %bitcast.57), channel_id=1, source_target_pairs={{0,23},{1,22},{2,21},{3,20},{4,19},{5,18},{6,17},{7,16},{8,31},{9,... | collective-permute-start | bytes 294920 | tf_op jit(solution)/shard_map/ppermute | solution.py:382
  72.0 4.2 %collective-permute-start.20 = (f32[16,256]{1,0:T(8,128)S(1)}, f32[16,256]{1,0:T(8,128)S(1)}, u32[]{:S(2)}, u32[]{:S(2)}) collective-permute-start(f32[16,256]{1,0:T(8,128)S(1)} %broadcast_select_fusion.refs_0_.refs_5_), channel_id=1, source_target_pairs={{0,4},{1,5},{2,6},{3,7},{4,0},{5,1},{6,2},{7,3},{8,12},{9,13},{10,... | collective-permute-start | bytes 49160 | tf_op jit(solution)/shard_map/ppermute | solution.py:382
  76.2 8.0 %collective-permute-start.10 = (f32[192,128]{1,0:T(8,128)}, f32[192,128]{1,0:T(8,128)S(1)}, u32[]{:S(2)}, u32[]{:S(2)}) collective-permute-start(f32[192,128]{1,0:T(8,128)} %bitcast.56), channel_id=1, source_target_pairs={{0,24},{1,25},{2,26},{3,27},{4,28},{5,29},{6,30},{7,31},{8,16},{9,... | collective-permute-start | bytes 294920 | tf_op jit(solution)/shard_map/ppermute | solution.py:382
  77.0 14.5 %collective-permute-start.11 = (f32[192,128]{1,0:T(8,128)}, f32[192,128]{1,0:T(8,128)S(1)}, u32[]{:S(2)}, u32[]{:S(2)}) collective-permute-start(f32[192,128]{1,0:T(8,128)} %bitcast.55), channel_id=1, source_target_pairs={{0,25},{1,24},{2,27},{3,26},{4,29},{5,28},{6,31},{7,30},{8,17},{9,... | collective-permute-start | bytes 294920 | tf_op jit(solution)/shard_map/ppermute | solution.py:382
  79.4 13.6 %collective-permute-start.12 = (f32[192,128]{1,0:T(8,128)}, f32[192,128]{1,0:T(8,128)S(1)}, u32[]{:S(2)}, u32[]{:S(2)}) collective-permute-start(f32[192,128]{1,0:T(8,128)} %bitcast.54), channel_id=1, source_target_pairs={{0,26},{1,27},{2,24},{3,25},{4,30},{5,31},{6,28},{7,29},{8,18},{9,... | collective-permute-start | bytes 294920 | tf_op jit(solution)/shard_map/ppermute | solution.py:382
  82.4 15.8 %collective-permute-start.13 = (f32[192,128]{1,0:T(8,128)}, f32[192,128]{1,0:T(8,128)S(1)}, u32[]{:S(2)}, u32[]{:S(2)}) collective-permute-start(f32[192,128]{1,0:T(8,128)} %bitcast.53), channel_id=1, source_target_pairs={{0,27},{1,26},{2,25},{3,24},{4,31},{5,30},{6,29},{7,28},{8,19},{9,... | collective-permute-start | bytes 294920 | tf_op jit(solution)/shard_map/ppermute | solution.py:382
  84.2 19.3 %collective-permute-start.27 = (f32[192,128]{1,0:T(8,128)}, f32[192,128]{1,0:T(8,128)S(1)}, u32[]{:S(2)}, u32[]{:S(2)}) collective-permute-start(f32[192,128]{1,0:T(8,128)} %bitcast.52), channel_id=1, source_target_pairs={{0,16},{1,17},{2,18},{3,19},{4,20},{5,21},{6,22},{7,23},{8,24},{9,... | collective-permute-start | bytes 294920 | tf_op jit(solution)/shard_map/ppermute | solution.py:382
  91.5 14.7 %collective-permute-start.28 = (f32[192,128]{1,0:T(8,128)}, f32[192,128]{1,0:T(8,128)S(1)}, u32[]{:S(2)}, u32[]{:S(2)}) collective-permute-start(f32[192,128]{1,0:T(8,128)} %bitcast.51), channel_id=1, source_target_pairs={{0,17},{1,16},{2,19},{3,18},{4,21},{5,20},{6,23},{7,22},{8,25},{9,... | collective-permute-start | bytes 294920 | tf_op jit(solution)/shard_map/ppermute | solution.py:382
  93.0 20.4 %collective-permute-start.29 = (f32[192,128]{1,0:T(8,128)}, f32[192,128]{1,0:T(8,128)S(1)}, u32[]{:S(2)}, u32[]{:S(2)}) collective-permute-start(f32[192,128]{1,0:T(8,128)} %bitcast.50), channel_id=1, source_target_pairs={{0,18},{1,19},{2,16},{3,17},{4,22},{5,23},{6,20},{7,21},{8,26},{9,... | collective-permute-start | bytes 294920 | tf_op jit(solution)/shard_map/ppermute | solution.py:382
  98.2 25.4 %collective-permute-start.26 = (f32[128,256]{1,0:T(8,128)}, f32[128,256]{1,0:T(8,128)S(1)}, u32[]{:S(2)}, u32[]{:S(2)}) collective-permute-start(f32[128,256]{1,0:T(8,128)} %stack.1), channel_id=1, source_target_pairs={{0,1},{1,0},{2,3},{3,2},{4,5},{5,4},{6,7},{7,6},{8,9},{9,8},{10,11... | collective-permute-start | bytes 393224 | tf_op jit(solution)/shard_map/ppermute | solution.py:382
  103.5 11.2 %collective-permute-start.30 = (f32[192,128]{1,0:T(8,128)}, f32[192,128]{1,0:T(8,128)S(1)}, u32[]{:S(2)}, u32[]{:S(2)}) collective-permute-start(f32[192,128]{1,0:T(8,128)} %bitcast.49), channel_id=1, source_target_pairs={{0,19},{1,18},{2,17},{3,16},{4,23},{5,22},{6,21},{7,20},{8,27},{9,... | collective-permute-start | bytes 294920 | tf_op jit(solution)/shard_map/ppermute | solution.py:382
  106.2 12.4 %collective-permute-start.31 = (f32[192,128]{1,0:T(8,128)}, f32[192,128]{1,0:T(8,128)S(1)}, u32[]{:S(2)}, u32[]{:S(2)}) collective-permute-start(f32[192,128]{1,0:T(8,128)} %bitcast.48), channel_id=1, source_target_pairs={{0,20},{1,21},{2,22},{3,23},{4,16},{5,17},{6,18},{7,19},{8,28},{9,... | collective-permute-start | bytes 294920 | tf_op jit(solution)/shard_map/ppermute | solution.py:382
  113.5 7.6 %collective-permute-start.32 = (f32[192,128]{1,0:T(8,128)}, f32[192,128]{1,0:T(8,128)S(1)}, u32[]{:S(2)}, u32[]{:S(2)}) collective-permute-start(f32[192,128]{1,0:T(8,128)} %bitcast.47), channel_id=1, source_target_pairs={{0,21},{1,20},{2,23},{3,22},{4,17},{5,16},{6,19},{7,18},{8,29},{9,... | collective-permute-start | bytes 294920 | tf_op jit(solution)/shard_map/ppermute | solution.py:382
  114.7 24.8 %collective-permute-start.14 = (f32[192,128]{1,0:T(8,128)}, f32[192,128]{1,0:T(8,128)S(1)}, u32[]{:S(2)}, u32[]{:S(2)}) collective-permute-start(f32[192,128]{1,0:T(8,128)} %bitcast.46), channel_id=1, source_target_pairs={{0,28},{1,29},{2,30},{3,31},{4,24},{5,25},{6,26},{7,27},{8,20},{9,... | collective-permute-start | bytes 294920 | tf_op jit(solution)/shard_map/ppermute | solution.py:382
  118.6 20.9 %collective-permute-start.15 = (f32[192,128]{1,0:T(8,128)}, f32[192,128]{1,0:T(8,128)S(1)}, u32[]{:S(2)}, u32[]{:S(2)}) collective-permute-start(f32[192,128]{1,0:T(8,128)} %bitcast.45), channel_id=1, source_target_pairs={{0,29},{1,28},{2,31},{3,30},{4,25},{5,24},{6,27},{7,26},{8,21},{9,... | collective-permute-start | bytes 294920 | tf_op jit(solution)/shard_map/ppermute | solution.py:382
  121.1 18.4 %collective-permute-start.16 = (f32[192,128]{1,0:T(8,128)}, f32[192,128]{1,0:T(8,128)S(1)}, u32[]{:S(2)}, u32[]{:S(2)}) collective-permute-start(f32[192,128]{1,0:T(8,128)} %bitcast.44), channel_id=1, source_target_pairs={{0,30},{1,31},{2,28},{3,29},{4,26},{5,27},{6,24},{7,25},{8,22},{9,... | collective-permute-start | bytes 294920 | tf_op jit(solution)/shard_map/ppermute | solution.py:382
  123.6 15.9 %collective-permute-start.17 = (f32[192,128]{1,0:T(8,128)}, f32[192,128]{1,0:T(8,128)S(1)}, u32[]{:S(2)}, u32[]{:S(2)}) collective-permute-start(f32[192,128]{1,0:T(8,128)} %bitcast.43), channel_id=1, source_target_pairs={{0,31},{1,30},{2,29},{3,28},{4,27},{5,26},{6,25},{7,24},{8,23},{9,... | collective-permute-start | bytes 294920 | tf_op jit(solution)/shard_map/ppermute | solution.py:382
  (26 other events, 449.6 us)
where the time goes:
time: 148 us; the launch traced here: 147 us
  starting transfers between devices  56.9 us (38%)
  waiting for transfers between devices  49 us (33%)
  Pallas kernels  38.7 us (26%)
  local copies, waits for them, and re-layouts  2.25 us (2%)
    ppermute x33, starting transfers between devices, exchange(): return lax.ppermute(x, 'dev', pairs)  49.6 us
    ppermute x33, waiting for transfers between devices, exchange(): return lax.ppermute(x, 'dev', pairs)  49 us
    pallas_call x2, Pallas kernels, whiten(): pl.pallas_call(functools.partial(whiten_kernel, rb=rb, groups=groups, out...  16.4 us
    pallas_call x1, Pallas kernels, finish(): pl.pallas_call(functools.partial(finish_kernel, rows=rows, parts=parts, s...  7.58 us
    all_to_all x1, starting transfers between devices, per_device(): head = lax.all_to_all(head, 'dev', 0, 0, tiled=True)  7.33 us
    pallas_call x1, Pallas kernels, solve(): pl.pallas_call(functools.partial(solve_kernel, rows=rows, parts=parts, pe...  7.15 us
    pallas_call x1, Pallas kernels, mix(): pl.pallas_call(functools.partial(mix_kernel, top=top, local=local, stages...  3.92 us
  transfers between devices with their start and end apart: 34, of which 16 were waited for; matrix products, arithmetic and copies ran while one was open for 0% of the time, Pallas kernels for 17%

commit v1 on v0

--- a/solution.py
+++ b/solution.py
@@ -295,57 +295,6 @@
     )(me, *args)
 
 
-def finish_kernel(me_ref, *refs, rows, parts, sizes):
-    n = len(sizes)
-    mh_ref, ml_ref, acc_ref, o_ref, held_ref, in_sems, out_sems = refs[n:]
-    span = parts * LANES
-    mh, ml = mh_ref[...], ml_ref[...]
-
-    def tile(ref, i):
-        return ref.at[:, i * span:(i + 1) * span]
-
-    def fetch(i):
-        return pltpu.make_async_copy(tile(acc_ref, i), held_ref.at[i], in_sems.at[i])
-
-    def store(i):
-        return pltpu.make_async_copy(held_ref.at[i], tile(o_ref, i), out_sems.at[i])
-
-    for i in range(rows):
-        fetch(i).start()
-    for i in range(rows):
-        columns = []
-        for p in range(parts):
-            column = [ref[pl.ds(p * rows + i, k, stride=rows * parts), :] for ref, k in zip(refs, sizes)]
-            columns.append(jnp.concatenate(column, axis=0))
-        wh, wl = split(jnp.concatenate(columns, axis=1))
-        out = mm(mh, wh) + mm(mh, wl) + mm(ml, wh)
-        fetch(i).wait()
-        held_ref[i] = held_ref[i] + out
-        store(i).start()
-    for i in range(rows):
-        store(i).wait()
-
-
-def finish(me, pieces, tables, rows, parts, acc):
-    each = rows * parts
-    width = tables[0].shape[0]
-    sizes = [a.shape[-2] // each for a in pieces]
-    args = [*pieces, *outside(tables)]
-    specs = [parity(a, False) if a.ndim == 3 else whole(a.shape) for a in args]
-    return pl.pallas_call(
-        functools.partial(finish_kernel, rows=rows, parts=parts, sizes=tuple(sizes)),
-        grid_spec=pltpu.PrefetchScalarGridSpec(
-            num_scalar_prefetch=1, grid=(1,), in_specs=[*specs, pl.BlockSpec(memory_space=pl.ANY)],
-            out_specs=pl.BlockSpec(memory_space=pl.ANY),
-            scratch_shapes=[pltpu.VMEM((rows, width, parts * LANES), jnp.float32),
-                            pltpu.SemaphoreType.DMA((rows,)), pltpu.SemaphoreType.DMA((rows,))]),
-        out_shape=jax.ShapeDtypeStruct((width, each * LANES), jnp.float32),
-        input_output_aliases={len(args) + 1: 0},
-        compiler_params=pltpu.CompilerParams(vmem_limit_bytes=24 << 20),
-        name="finish",
-    )(me, *args, acc)
-
-
 def precise_dot(a, b):
     return jnp.dot(a, b, precision=lax.Precision.HIGHEST, preferred_element_type=jnp.float32)
 
@@ -424,7 +373,7 @@
     near = list(range(1, chips // 2))
     mine = factor_panels[0]
     mine = jnp.where(place < top, exchange(mine, top), mine)
-    (head,) = whiten(me, runs_field, spectral_filter, groups, 0, HEAD, HEAD // 2, False)
+    (head,) = whiten(me, runs_field, spectral_filter, groups, 0, HEAD, HEAD, False)
     head = lax.all_to_all(head, "dev", 0, 0, tiled=True)
     outs = whiten(me, runs_field, spectral_filter, groups, HEAD, rest, HEAD, True)
     got = [outs[0].reshape(2, -1, LANES)]
@@ -441,7 +390,7 @@
     load = bundle(me, got)
     load = exchange(load, 1)
     out = solve(me, outside([head.reshape(-1, LANES), *got[:NEAR_SOON], *direct[:SOON]]), tables[:2], rows, parts)
-    return finish(me, [load, *outside(got[NEAR_SOON:]), *direct[SOON:]], tables[2:], rows, parts, out)
+    return solve(me, [load, *outside(got[NEAR_SOON:]), *direct[SOON:]], tables[2:], rows, parts, out)
 
 
 def solution(mesh):

time: 148 us -> 145 us (0.980)
  Pallas kernels: 38.7 us -> 36.3 us
    pallas_call x1 -> x0, Pallas kernels: 7.58 us -> none  [finish(): pl.pallas_call(functools.partial(finish_kernel, rows=rows, parts=parts, s...]
    pallas_call x1 -> x2, Pallas kernels: 7.15 us -> 12.6 us  [solve(): pl.pallas_call(functools.partial(solve_kernel, rows=rows, parts=parts, pe...]
  transfers between devices with their start and end apart: 34 -> 34, of which waited for: 16 -> 16; matrix products, arithmetic and copies ran while one was open for 0% -> 0% of each run, Pallas kernels for 17% -> 18%
where the time goes in v1:
time: 145 us
  starting transfers between devices  57.7 us (40%)
  waiting for transfers between devices  48.2 us (33%)
  Pallas kernels  36.3 us (25%)
  local copies, waits for them, and re-layouts  2.25 us (2%)
    ppermute x33, starting transfers between devices, exchange(): return lax.ppermute(x, 'dev', pairs)  50.2 us
    ppermute x33, waiting for transfers between devices, exchange(): return lax.ppermute(x, 'dev', pairs)  48.2 us
    pallas_call x2, Pallas kernels, whiten(): pl.pallas_call(functools.partial(whiten_kernel, rb=rb, groups=groups, out...  16.1 us
    pallas_call x2, Pallas kernels, solve(): pl.pallas_call(functools.partial(solve_kernel, rows=rows, parts=parts, pe...  12.6 us
    all_to_all x1, starting transfers between devices, per_device(): head = lax.all_to_all(head, 'dev', 0, 0, tiled=True)  7.5 us
    pallas_call x1, Pallas kernels, mix(): pl.pallas_call(functools.partial(mix_kernel, top=top, local=local, stages...  3.92 us
  transfers between devices with their start and end apart: 34, of which 16 were waited for; matrix products, arithmetic and copies ran while one was open for 0% of the time, Pallas kernels for 18%

profile of v1, /device:TPU:0, one launch (start us, length us, event | category | flops | bytes accessed | tf_op | source)
XLA Modules:
  0.0 144.7 jit_solution(8740051956982312229)
XLA Ops:
  0.0 5.3 %whiten.3 = f32[32,4,2,8,128]{4,3,2,1,0:T(8,128)} custom-call(s32[1]{0:T(128)} %bitcast.me_ref, f32[16,256,256]{2,1,0:T(8,128)} %x_ref.3, f32[129,256]{1,0:T(8,128)} %bitcast.34, bf16[256,256]{1,0:T(8,128)(2,1)} %constant.30.clone.rest_0_, bf16[256,256]{1,0:T(8,128)(2,1)} %constant.31.clone.rest_1_, bf16[256,256]{1,0:T(8,128)(2,1)} %constant.32.clone.rest_2_, ...), custom_call_target="tpu_custom_call" | custom-call | tf_op jit(solution)/shard_map/whiten/pallas_call | solution.py:139
  5.3 7.5 %all-to-all-start = ((f32[32,4,2,8,128]{4,3,2,1,0:T(8,128)}), f32[32,4,2,8,128]{4,3,2,1,0:T(8,128)S(1)}, u32[]{:S(2)}, u32[]{:S(2)}) async-start(f32[32,4,2,8,128]{4,3,2,1,0:T(8,128)} %whiten.3), calls=%async_computation | async-start | bytes 2097152 | tf_op jit(solution)/shard_map/all_to_all | solution.py:377
  12.9 10.7 %whiten.2 = (f32[2,12,2,8,128]{4,3,2,1,0:T(8,128)}, f32[2,12,2,8,128]{4,3,2,1,0:T(8,128)}, f32[2,12,2,8,128]{4,3,2,1,0:T(8,128)}, f32[2,12,2,8,128]{4,3,2,1,0:T(...) custom-call(s32[1]{0:T(128)} %bitcast.me_ref, ...), custom_call_target="tpu_custom_call" | custom-call | tf_op jit(solution)/shard_map/whiten/pallas_call | solution.py:139
  30.2 2.8 %collective-permute-done.refs_1_.refs_2_ = f32[2,192,128]{2,1,0:T(8,128)S(1)} collective-permute-done((f32[2,192,128]{2,1,0:T(8,128)}, f32[2,192,128]{2,1,0:T(8,128)S(1)}, u32[]{:S(2)}, u32[]{:S(2)}) %collective-permute-start) | collective-permute-done | bytes 196640 | tf_op jit(solution)/shard_map/ppermute | solution.py:331
  33.0 2.9 %collective-permute-start.5 = (f32[2,192,128]{2,1,0:T(8,128)}, f32[2,192,128]{2,1,0:T(8,128)S(1)}, u32[]{:S(2)}, u32[]{:S(2)}) collective-permute-start(f32[2,192,128]{2,1,0:T(8,128)} %bitcast.37), channel_id=1, source_target_pairs={{0,12},{1,13},{2,14},{3,15},{4,8},{5,9},{6,10},{7,11},{8,4},{9,5},... | collective-permute-start | bytes 589832 | tf_op jit(solution)/shard_map/ppermute | solution.py:331
  35.9 2.8 %collective-permute-done.1.refs_2_.refs_3_ = f32[2,192,128]{2,1,0:T(8,128)S(1)} collective-permute-done((f32[2,192,128]{2,1,0:T(8,128)}, f32[2,192,128]{2,1,0:T(8,128)S(1)}, u32[]{:S(2)}, u32[]{:S(2)}) %collective-permute-start.1) | collective-permute-done | bytes 196640 | tf_op jit(solution)/shard_map/ppermute | solution.py:331
  39.9 4.4 %collective-permute-done.4.refs_5_.refs_1_ = f32[2,192,128]{2,1,0:T(8,128)S(1)} collective-permute-done((f32[2,192,128]{2,1,0:T(8,128)}, f32[2,192,128]{2,1,0:T(8,128)S(1)}, u32[]{:S(2)}, u32[]{:S(2)}) %collective-permute-start.4) | collective-permute-done | bytes 196640 | tf_op jit(solution)/shard_map/ppermute | solution.py:331
  44.3 4.1 %collective-permute-done.5.refs_6_.refs_2_ = f32[2,192,128]{2,1,0:T(8,128)S(1)} collective-permute-done((f32[2,192,128]{2,1,0:T(8,128)}, f32[2,192,128]{2,1,0:T(8,128)S(1)}, u32[]{:S(2)}, u32[]{:S(2)}) %collective-permute-start.5) | collective-permute-done | bytes 196640 | tf_op jit(solution)/shard_map/ppermute | solution.py:331
  48.4 4.6 %collective-permute-done.6.refs_7_.refs_3_ = f32[2,192,128]{2,1,0:T(8,128)S(1)} collective-permute-done((f32[2,192,128]{2,1,0:T(8,128)}, f32[2,192,128]{2,1,0:T(8,128)S(1)}, u32[]{:S(2)}, u32[]{:S(2)}) %collective-permute-start.6) | collective-permute-done | bytes 196640 | tf_op jit(solution)/shard_map/ppermute | solution.py:331
  53.7 2.2 %bundle.1 = f32[1536,128]{1,0:T(8,128)} custom-call(s32[1]{0:T(128)} %bitcast.me_ref, f32[2,192,128]{2,1,0:T(8,128)} %bitcast.32, f32[2,192,128]{2,1,0:T(8,128)} %copy-done.4, f32[2,192,128]{2,1,0:T(8,128)} %copy-done.5, f32[2,192,128]{2,1,0:T(8,128)} %copy-done.6, f32[2,192,128]{2,1,0:T(8,128)} %copy-done.7, f32[2,192,128]{2,1,0:T(8,128)} %copy-done.1, ...), custom_call_target="tpu_custom_call" | custom-call | tf_op jit(solution)/shard_map/bundle/pallas_call | solution.py:197
  55.9 1.9 %collective-permute-start.18 = (f32[16,256]{1,0:T(8,128)S(1)}, f32[16,256]{1,0:T(8,128)S(1)}, u32[]{:S(2)}, u32[]{:S(2)}) collective-permute-start(f32[16,256]{1,0:T(8,128)S(1)} %slice_bitcast_fusion), channel_id=1, source_target_pairs={{0,16},{1,17},{2,18},{3,19},{4,20},{5,21},{6,22},{7,23},{8,24},{9,... | collective-permute-start | bytes 49160 | tf_op jit(solution)/shard_map/ppermute | solution.py:331
  58.5 2.3 %collective-permute-done.18 = f32[16,256]{1,0:T(8,128)S(1)} collective-permute-done((f32[16,256]{1,0:T(8,128)S(1)}, f32[16,256]{1,0:T(8,128)S(1)}, u32[]{:S(2)}, u32[]{:S(2)}) %collective-permute-start.18) | collective-permute-done | bytes 16416 | tf_op jit(solution)/shard_map/ppermute | solution.py:331
  61.6 2.1 %collective-permute-start.24 = (f32[16,256]{1,0:T(8,128)S(1)}, f32[16,256]{1,0:T(8,128)S(1)}, u32[]{:S(2)}, u32[]{:S(2)}) collective-permute-start(f32[16,256]{1,0:T(8,128)S(1)} %broadcast_select_fusion.refs_0_.refs_5_), channel_id=1, source_target_pairs={{0,12},{1,13},{2,14},{3,15},{4,8},{5,9},{6,10},{7,11},{8,4},{9,5},... | collective-permute-start | bytes 49160 | tf_op jit(solution)/shard_map/ppermute | solution.py:331
  65.0 3.0 %collective-permute-done.25.refs_7_.refs_12_ = f32[16,256]{1,0:T(8,128)S(1)} collective-permute-done((f32[16,256]{1,0:T(8,128)S(1)}, f32[16,256]{1,0:T(8,128)S(1)}, u32[]{:S(2)}, u32[]{:S(2)}) %collective-permute-start.25) | collective-permute-done | bytes 16416 | tf_op jit(solution)/shard_map/ppermute | solution.py:331
  68.7 3.0 %collective-permute-done.22.refs_4_.refs_9_ = f32[16,256]{1,0:T(8,128)S(1)} collective-permute-done((f32[16,256]{1,0:T(8,128)S(1)}, f32[16,256]{1,0:T(8,128)S(1)}, u32[]{:S(2)}, u32[]{:S(2)}) %collective-permute-start.22) | collective-permute-done | bytes 16416 | tf_op jit(solution)/shard_map/ppermute | solution.py:331
  73.5 2.4 %collective-permute-done.20.refs_2_.refs_7_ = f32[16,256]{1,0:T(8,128)S(1)} collective-permute-done((f32[16,256]{1,0:T(8,128)S(1)}, f32[16,256]{1,0:T(8,128)S(1)}, u32[]{:S(2)}, u32[]{:S(2)}) %collective-permute-start.20) | collective-permute-done | bytes 16416 | tf_op jit(solution)/shard_map/ppermute | solution.py:331
  76.7 2.4 %collective-permute-start.11 = (f32[192,128]{1,0:T(8,128)}, f32[192,128]{1,0:T(8,128)S(1)}, u32[]{:S(2)}, u32[]{:S(2)}) collective-permute-start(f32[192,128]{1,0:T(8,128)} %bitcast.55), channel_id=1, source_target_pairs={{0,25},{1,24},{2,27},{3,26},{4,29},{5,28},{6,31},{7,30},{8,17},{9,... | collective-permute-start | bytes 294920 | tf_op jit(solution)/shard_map/ppermute | solution.py:331
  79.1 2.9 %collective-permute-start.12 = (f32[192,128]{1,0:T(8,128)}, f32[192,128]{1,0:T(8,128)S(1)}, u32[]{:S(2)}, u32[]{:S(2)}) collective-permute-start(f32[192,128]{1,0:T(8,128)} %bitcast.54), channel_id=1, source_target_pairs={{0,26},{1,27},{2,24},{3,25},{4,30},{5,31},{6,28},{7,29},{8,18},{9,... | collective-permute-start | bytes 294920 | tf_op jit(solution)/shard_map/ppermute | solution.py:331
  82.0 1.8 %collective-permute-start.13 = (f32[192,128]{1,0:T(8,128)}, f32[192,128]{1,0:T(8,128)S(1)}, u32[]{:S(2)}, u32[]{:S(2)}) collective-permute-start(f32[192,128]{1,0:T(8,128)} %bitcast.53), channel_id=1, source_target_pairs={{0,27},{1,26},{2,25},{3,24},{4,31},{5,30},{6,29},{7,28},{8,19},{9,... | collective-permute-start | bytes 294920 | tf_op jit(solution)/shard_map/ppermute | solution.py:331
  83.9 7.3 %collective-permute-start.27 = (f32[192,128]{1,0:T(8,128)}, f32[192,128]{1,0:T(8,128)S(1)}, u32[]{:S(2)}, u32[]{:S(2)}) collective-permute-start(f32[192,128]{1,0:T(8,128)} %bitcast.52), channel_id=1, source_target_pairs={{0,16},{1,17},{2,18},{3,19},{4,20},{5,21},{6,22},{7,23},{8,24},{9,... | collective-permute-start | bytes 294920 | tf_op jit(solution)/shard_map/ppermute | solution.py:331
  92.7 3.6 %collective-permute-start.29 = (f32[192,128]{1,0:T(8,128)}, f32[192,128]{1,0:T(8,128)S(1)}, u32[]{:S(2)}, u32[]{:S(2)}) collective-permute-start(f32[192,128]{1,0:T(8,128)} %bitcast.50), channel_id=1, source_target_pairs={{0,18},{1,19},{2,16},{3,17},{4,22},{5,23},{6,20},{7,21},{8,26},{9,... | collective-permute-start | bytes 294920 | tf_op jit(solution)/shard_map/ppermute | solution.py:331
  97.9 5.2 %collective-permute-done.27.refs_6_ = f32[192,128]{1,0:T(8,128)S(1)} collective-permute-done((f32[192,128]{1,0:T(8,128)}, f32[192,128]{1,0:T(8,128)S(1)}, u32[]{:S(2)}, u32[]{:S(2)}) %collective-permute-start.27) | collective-permute-done | bytes 98336 | tf_op jit(solution)/shard_map/ppermute | solution.py:331
  103.4 2.5 %collective-permute-done.28.refs_7_ = f32[192,128]{1,0:T(8,128)S(1)} collective-permute-done((f32[192,128]{1,0:T(8,128)}, f32[192,128]{1,0:T(8,128)S(1)}, u32[]{:S(2)}, u32[]{:S(2)}) %collective-permute-start.28) | collective-permute-done | bytes 98336 | tf_op jit(solution)/shard_map/ppermute | solution.py:331
  106.2 7.1 %collective-permute-done.29.refs_8_ = f32[192,128]{1,0:T(8,128)S(1)} collective-permute-done((f32[192,128]{1,0:T(8,128)}, f32[192,128]{1,0:T(8,128)S(1)}, u32[]{:S(2)}, u32[]{:S(2)}) %collective-permute-start.29) | collective-permute-done | bytes 98336 | tf_op jit(solution)/shard_map/ppermute | solution.py:331
  113.3 2.0 %collective-permute-done.30.refs_9_ = f32[192,128]{1,0:T(8,128)S(1)} collective-permute-done((f32[192,128]{1,0:T(8,128)}, f32[192,128]{1,0:T(8,128)S(1)}, u32[]{:S(2)}, u32[]{:S(2)}) %collective-permute-start.30) | collective-permute-done | bytes 98336 | tf_op jit(solution)/shard_map/ppermute | solution.py:331
  115.4 2.3 %collective-permute-start.14 = (f32[192,128]{1,0:T(8,128)}, f32[192,128]{1,0:T(8,128)S(1)}, u32[]{:S(2)}, u32[]{:S(2)}) collective-permute-start(f32[192,128]{1,0:T(8,128)} %bitcast.46), channel_id=1, source_target_pairs={{0,28},{1,29},{2,30},{3,31},{4,24},{5,25},{6,26},{7,27},{8,20},{9,... | collective-permute-start | bytes 294920 | tf_op jit(solution)/shard_map/ppermute | solution.py:331
  118.1 2.7 %collective-permute-start.15 = (f32[192,128]{1,0:T(8,128)}, f32[192,128]{1,0:T(8,128)S(1)}, u32[]{:S(2)}, u32[]{:S(2)}) collective-permute-start(f32[192,128]{1,0:T(8,128)} %bitcast.45), channel_id=1, source_target_pairs={{0,29},{1,28},{2,31},{3,30},{4,25},{5,24},{6,27},{7,26},{8,21},{9,... | collective-permute-start | bytes 294920 | tf_op jit(solution)/shard_map/ppermute | solution.py:331
  120.8 2.5 %collective-permute-start.16 = (f32[192,128]{1,0:T(8,128)}, f32[192,128]{1,0:T(8,128)S(1)}, u32[]{:S(2)}, u32[]{:S(2)}) collective-permute-start(f32[192,128]{1,0:T(8,128)} %bitcast.44), channel_id=1, source_target_pairs={{0,30},{1,31},{2,28},{3,29},{4,26},{5,27},{6,24},{7,25},{8,22},{9,... | collective-permute-start | bytes 294920 | tf_op jit(solution)/shard_map/ppermute | solution.py:331
  123.3 3.2 %collective-permute-start.17 = (f32[192,128]{1,0:T(8,128)}, f32[192,128]{1,0:T(8,128)S(1)}, u32[]{:S(2)}, u32[]{:S(2)}) collective-permute-start(f32[192,128]{1,0:T(8,128)} %bitcast.43), channel_id=1, source_target_pairs={{0,31},{1,30},{2,29},{3,28},{4,27},{5,26},{6,25},{7,24},{8,23},{9,... | collective-permute-start | bytes 294920 | tf_op jit(solution)/shard_map/ppermute | solution.py:331
  127.1 3.9 %mix.1 = (bf16[512,260]{1,0:T(8,128)(2,1)}, bf16[512,260]{1,0:T(8,128)(2,1)}, bf16[512,252]{1,0:T(8,128)(2,1)}, bf16[512,252]{1,0:T(8,128)(2,1)}) custom-call(s32[1]{0:T(128)} %bitcast.me_ref, s32[1,260]{1,0:T(1,128)} %constant.38.clone.refs_0_, s32[1,260]{1,0:T(1,128)} %constant.39.clone.refs_1_, s32[1,252]{1,0:T(1,128)} %constant.40.clone.refs_2_, ...), custom_call_target="tpu_custom_call" | custom-call | tf_op jit(solution)/shard_map/mix/pallas_call | solution.py:248
  132.1 7.1 %solve.2.refs_16_ = f32[512,2048]{1,0:T(8,128)} custom-call(s32[1]{0:T(128)} %bitcast.me_ref, f32[2048,128]{1,0:T(8,128)} %bitcast.31, f32[2,192,128]{2,1,0:T(8,128)} %bitcast.33, f32[2,192,128]{2,1,0:T(8,128)} %copy-done.4, f32[2,192,128]{2,1,0:T(8,128)} %copy-done.5, f32[2,192,128]{2,1,0:T(8,128)} %copy-done.6, f32[2,192,128]{2,1,0:T(8,128)} %copy-done.7, ...), custom_call_target="tpu_custom_call" | custom-call | tf_op jit(solution)/shard_map/solve/pallas_call | solution.py:287
  139.2 5.5 %solve.3 = f32[512,2048]{1,0:T(8,128)} custom-call(s32[1]{0:T(128)} %bitcast.me_ref, f32[1536,128]{1,0:T(8,128)S(1)} %collective-permute-done.7.refs_0_, f32[2,192,128]{2,1,0:T(8,128)} %copy-done.1, f32[2,192,128]{2,1,0:T(8,128)} %copy-done.2, f32[2,192,128]{2,1,0:T(8,128)} %copy-done.3, ...), custom_call_target="tpu_custom_call", output_to_operand_aliasing={{}: (17, {})} | custom-call | tf_op jit(solution)/shard_map/solve/pallas_call | solution.py:287
  (94 shorter events, 20.3 us)
Async XLA Ops:
  5.3 125.7 %all-to-all-start = ((f32[32,4,2,8,128]{4,3,2,1,0:T(8,128)}), f32[32,4,2,8,128]{4,3,2,1,0:T(8,128)S(1)}, u32[]{:S(2)}, u32[]{:S(2)}) async-start(f32[32,4,2,8,128]{4,3,2,1,0:T(8,128)} %whiten.3), calls=%async_computation | async-start | bytes 2097152 | tf_op jit(solution)/shard_map/all_to_all | solution.py:377
  23.6 9.4 %collective-permute-start = (f32[2,192,128]{2,1,0:T(8,128)}, f32[2,192,128]{2,1,0:T(8,128)S(1)}, u32[]{:S(2)}, u32[]{:S(2)}) collective-permute-start(f32[2,192,128]{2,1,0:T(8,128)} %bitcast.42), channel_id=1, source_target_pairs={{0,2},{1,3},{2,0},{3,1},{4,6},{5,7},{6,4},{7,5},{8,10},{9,11},{10,... | collective-permute-start | bytes 589832 | tf_op jit(solution)/shard_map/ppermute | solution.py:331
  25.3 13.5 %collective-permute-start.1 = (f32[2,192,128]{2,1,0:T(8,128)}, f32[2,192,128]{2,1,0:T(8,128)S(1)}, u32[]{:S(2)}, u32[]{:S(2)}) collective-permute-start(f32[2,192,128]{2,1,0:T(8,128)} %bitcast.41), channel_id=1, source_target_pairs={{0,4},{1,5},{2,6},{3,7},{4,0},{5,1},{6,2},{7,3},{8,12},{9,13},{10,... | collective-permute-start | bytes 589832 | tf_op jit(solution)/shard_map/ppermute | solution.py:331
  26.7 13.1 %collective-permute-start.2 = (f32[2,192,128]{2,1,0:T(8,128)}, f32[2,192,128]{2,1,0:T(8,128)S(1)}, u32[]{:S(2)}, u32[]{:S(2)}) collective-permute-start(f32[2,192,128]{2,1,0:T(8,128)} %bitcast.40), channel_id=1, source_target_pairs={{0,6},{1,7},{2,4},{3,5},{4,2},{5,3},{6,0},{7,1},{8,14},{9,15},{10,... | collective-permute-start | bytes 589832 | tf_op jit(solution)/shard_map/ppermute | solution.py:331
  27.2 12.7 %collective-permute-start.3 = (f32[2,192,128]{2,1,0:T(8,128)}, f32[2,192,128]{2,1,0:T(8,128)S(1)}, u32[]{:S(2)}, u32[]{:S(2)}) collective-permute-start(f32[2,192,128]{2,1,0:T(8,128)} %bitcast.39), channel_id=1, source_target_pairs={{0,8},{1,9},{2,10},{3,11},{4,12},{5,13},{6,14},{7,15},{8,0},{9,1},... | collective-permute-start | bytes 589832 | tf_op jit(solution)/shard_map/ppermute | solution.py:331
  28.8 15.5 %collective-permute-start.4 = (f32[2,192,128]{2,1,0:T(8,128)}, f32[2,192,128]{2,1,0:T(8,128)S(1)}, u32[]{:S(2)}, u32[]{:S(2)}) collective-permute-start(f32[2,192,128]{2,1,0:T(8,128)} %bitcast.38), channel_id=1, source_target_pairs={{0,10},{1,11},{2,8},{3,9},{4,14},{5,15},{6,12},{7,13},{8,2},{9,3},... | collective-permute-start | bytes 589832 | tf_op jit(solution)/shard_map/ppermute | solution.py:331
  33.0 15.4 %collective-permute-start.5 = (f32[2,192,128]{2,1,0:T(8,128)}, f32[2,192,128]{2,1,0:T(8,128)S(1)}, u32[]{:S(2)}, u32[]{:S(2)}) collective-permute-start(f32[2,192,128]{2,1,0:T(8,128)} %bitcast.37), channel_id=1, source_target_pairs={{0,12},{1,13},{2,14},{3,15},{4,8},{5,9},{6,10},{7,11},{8,4},{9,5},... | collective-permute-start | bytes 589832 | tf_op jit(solution)/shard_map/ppermute | solution.py:331
  38.8 14.2 %collective-permute-start.6 = (f32[2,192,128]{2,1,0:T(8,128)}, f32[2,192,128]{2,1,0:T(8,128)S(1)}, u32[]{:S(2)}, u32[]{:S(2)}) collective-permute-start(f32[2,192,128]{2,1,0:T(8,128)} %bitcast.36), channel_id=1, source_target_pairs={{0,14},{1,15},{2,12},{3,13},{4,10},{5,11},{6,8},{7,9},{8,6},{9,7},... | collective-permute-start | bytes 589832 | tf_op jit(solution)/shard_map/ppermute | solution.py:331
  55.9 83.4 %collective-permute-start.7 = (f32[1536,128]{1,0:T(8,128)}, f32[1536,128]{1,0:T(8,128)S(1)}, u32[]{:S(2)}, u32[]{:S(2)}) collective-permute-start(f32[1536,128]{1,0:T(8,128)} %bundle.1), channel_id=1, source_target_pairs={{0,1},{1,0},{2,3},{3,2},{4,5},{5,4},{6,7},{7,6},{8,9},{9,8},{10,11... | collective-permute-start | bytes 2359304 | tf_op jit(solution)/shard_map/ppermute | solution.py:331
  55.9 4.9 %collective-permute-start.18 = (f32[16,256]{1,0:T(8,128)S(1)}, f32[16,256]{1,0:T(8,128)S(1)}, u32[]{:S(2)}, u32[]{:S(2)}) collective-permute-start(f32[16,256]{1,0:T(8,128)S(1)} %slice_bitcast_fusion), channel_id=1, source_target_pairs={{0,16},{1,17},{2,18},{3,19},{4,20},{5,21},{6,22},{7,23},{8,24},{9,... | collective-permute-start | bytes 49160 | tf_op jit(solution)/shard_map/ppermute | solution.py:331
  57.8 21.4 %collective-permute-start.8 = (f32[192,128]{1,0:T(8,128)}, f32[192,128]{1,0:T(8,128)S(1)}, u32[]{:S(2)}, u32[]{:S(2)}) collective-permute-start(f32[192,128]{1,0:T(8,128)} %bitcast.58), channel_id=1, source_target_pairs={{0,22},{1,23},{2,20},{3,21},{4,18},{5,19},{6,16},{7,17},{8,30},{9,... | collective-permute-start | bytes 294920 | tf_op jit(solution)/shard_map/ppermute | solution.py:331
  60.8 7.2 %collective-permute-start.25 = (f32[16,256]{1,0:T(8,128)S(1)}, f32[16,256]{1,0:T(8,128)S(1)}, u32[]{:S(2)}, u32[]{:S(2)}) collective-permute-start(f32[16,256]{1,0:T(8,128)S(1)} %broadcast_select_fusion.refs_0_.refs_5_), channel_id=1, source_target_pairs={{0,14},{1,15},{2,12},{3,13},{4,10},{5,11},{6,8},{7,9},{8,6},{9,7},... | collective-permute-start | bytes 49160 | tf_op jit(solution)/shard_map/ppermute | solution.py:331
  61.6 6.4 %collective-permute-start.24 = (f32[16,256]{1,0:T(8,128)S(1)}, f32[16,256]{1,0:T(8,128)S(1)}, u32[]{:S(2)}, u32[]{:S(2)}) collective-permute-start(f32[16,256]{1,0:T(8,128)S(1)} %broadcast_select_fusion.refs_0_.refs_5_), channel_id=1, source_target_pairs={{0,12},{1,13},{2,14},{3,15},{4,8},{5,9},{6,10},{7,11},{8,4},{9,5},... | collective-permute-start | bytes 49160 | tf_op jit(solution)/shard_map/ppermute | solution.py:331
  63.7 5.1 %collective-permute-start.23 = (f32[16,256]{1,0:T(8,128)S(1)}, f32[16,256]{1,0:T(8,128)S(1)}, u32[]{:S(2)}, u32[]{:S(2)}) collective-permute-start(f32[16,256]{1,0:T(8,128)S(1)} %broadcast_select_fusion.refs_0_.refs_5_), channel_id=1, source_target_pairs={{0,10},{1,11},{2,8},{3,9},{4,14},{5,15},{6,12},{7,13},{8,2},{9,3},... | collective-permute-start | bytes 49160 | tf_op jit(solution)/shard_map/ppermute | solution.py:331
  68.0 4.7 %collective-permute-start.21 = (f32[16,256]{1,0:T(8,128)S(1)}, f32[16,256]{1,0:T(8,128)S(1)}, u32[]{:S(2)}, u32[]{:S(2)}) collective-permute-start(f32[16,256]{1,0:T(8,128)S(1)} %broadcast_select_fusion.refs_0_.refs_5_), channel_id=1, source_target_pairs={{0,6},{1,7},{2,4},{3,5},{4,2},{5,3},{6,0},{7,1},{8,14},{9,15},{10,... | collective-permute-start | bytes 49160 | tf_op jit(solution)/shard_map/ppermute | solution.py:331
  68.7 13.3 %collective-permute-start.9 = (f32[192,128]{1,0:T(8,128)}, f32[192,128]{1,0:T(8,128)S(1)}, u32[]{:S(2)}, u32[]{:S(2)}) collective-permute-start(f32[192,128]{1,0:T(8,128)} %bitcast.57), channel_id=1, source_target_pairs={{0,23},{1,22},{2,21},{3,20},{4,19},{5,18},{6,17},{7,16},{8,31},{9,... | collective-permute-start | bytes 294920 | tf_op jit(solution)/shard_map/ppermute | solution.py:331
  71.7 4.2 %collective-permute-start.20 = (f32[16,256]{1,0:T(8,128)S(1)}, f32[16,256]{1,0:T(8,128)S(1)}, u32[]{:S(2)}, u32[]{:S(2)}) collective-permute-start(f32[16,256]{1,0:T(8,128)S(1)} %broadcast_select_fusion.refs_0_.refs_5_), channel_id=1, source_target_pairs={{0,4},{1,5},{2,6},{3,7},{4,0},{5,1},{6,2},{7,3},{8,12},{9,13},{10,... | collective-permute-start | bytes 49160 | tf_op jit(solution)/shard_map/ppermute | solution.py:331
  75.9 8.0 %collective-permute-start.10 = (f32[192,128]{1,0:T(8,128)}, f32[192,128]{1,0:T(8,128)S(1)}, u32[]{:S(2)}, u32[]{:S(2)}) collective-permute-start(f32[192,128]{1,0:T(8,128)} %bitcast.56), channel_id=1, source_target_pairs={{0,24},{1,25},{2,26},{3,27},{4,28},{5,29},{6,30},{7,31},{8,16},{9,... | collective-permute-start | bytes 294920 | tf_op jit(solution)/shard_map/ppermute | solution.py:331
  76.7 14.5 %collective-permute-start.11 = (f32[192,128]{1,0:T(8,128)}, f32[192,128]{1,0:T(8,128)S(1)}, u32[]{:S(2)}, u32[]{:S(2)}) collective-permute-start(f32[192,128]{1,0:T(8,128)} %bitcast.55), channel_id=1, source_target_pairs={{0,25},{1,24},{2,27},{3,26},{4,29},{5,28},{6,31},{7,30},{8,17},{9,... | collective-permute-start | bytes 294920 | tf_op jit(solution)/shard_map/ppermute | solution.py:331
  79.1 13.6 %collective-permute-start.12 = (f32[192,128]{1,0:T(8,128)}, f32[192,128]{1,0:T(8,128)S(1)}, u32[]{:S(2)}, u32[]{:S(2)}) collective-permute-start(f32[192,128]{1,0:T(8,128)} %bitcast.54), channel_id=1, source_target_pairs={{0,26},{1,27},{2,24},{3,25},{4,30},{5,31},{6,28},{7,29},{8,18},{9,... | collective-permute-start | bytes 294920 | tf_op jit(solution)/shard_map/ppermute | solution.py:331
  82.0 15.8 %collective-permute-start.13 = (f32[192,128]{1,0:T(8,128)}, f32[192,128]{1,0:T(8,128)S(1)}, u32[]{:S(2)}, u32[]{:S(2)}) collective-permute-start(f32[192,128]{1,0:T(8,128)} %bitcast.53), channel_id=1, source_target_pairs={{0,27},{1,26},{2,25},{3,24},{4,31},{5,30},{6,29},{7,28},{8,19},{9,... | collective-permute-start | bytes 294920 | tf_op jit(solution)/shard_map/ppermute | solution.py:331
  83.9 19.2 %collective-permute-start.27 = (f32[192,128]{1,0:T(8,128)}, f32[192,128]{1,0:T(8,128)S(1)}, u32[]{:S(2)}, u32[]{:S(2)}) collective-permute-start(f32[192,128]{1,0:T(8,128)} %bitcast.52), channel_id=1, source_target_pairs={{0,16},{1,17},{2,18},{3,19},{4,20},{5,21},{6,22},{7,23},{8,24},{9,... | collective-permute-start | bytes 294920 | tf_op jit(solution)/shard_map/ppermute | solution.py:331
  91.2 14.7 %collective-permute-start.28 = (f32[192,128]{1,0:T(8,128)}, f32[192,128]{1,0:T(8,128)S(1)}, u32[]{:S(2)}, u32[]{:S(2)}) collective-permute-start(f32[192,128]{1,0:T(8,128)} %bitcast.51), channel_id=1, source_target_pairs={{0,17},{1,16},{2,19},{3,18},{4,21},{5,20},{6,23},{7,22},{8,25},{9,... | collective-permute-start | bytes 294920 | tf_op jit(solution)/shard_map/ppermute | solution.py:331
  92.7 20.6 %collective-permute-start.29 = (f32[192,128]{1,0:T(8,128)}, f32[192,128]{1,0:T(8,128)S(1)}, u32[]{:S(2)}, u32[]{:S(2)}) collective-permute-start(f32[192,128]{1,0:T(8,128)} %bitcast.50), channel_id=1, source_target_pairs={{0,18},{1,19},{2,16},{3,17},{4,22},{5,23},{6,20},{7,21},{8,26},{9,... | collective-permute-start | bytes 294920 | tf_op jit(solution)/shard_map/ppermute | solution.py:331
  97.9 25.4 %collective-permute-start.26 = (f32[128,256]{1,0:T(8,128)}, f32[128,256]{1,0:T(8,128)S(1)}, u32[]{:S(2)}, u32[]{:S(2)}) collective-permute-start(f32[128,256]{1,0:T(8,128)} %stack.1), channel_id=1, source_target_pairs={{0,1},{1,0},{2,3},{3,2},{4,5},{5,4},{6,7},{7,6},{8,9},{9,8},{10,11... | collective-permute-start | bytes 393224 | tf_op jit(solution)/shard_map/ppermute | solution.py:331
  103.1 12.3 %collective-permute-start.30 = (f32[192,128]{1,0:T(8,128)}, f32[192,128]{1,0:T(8,128)S(1)}, u32[]{:S(2)}, u32[]{:S(2)}) collective-permute-start(f32[192,128]{1,0:T(8,128)} %bitcast.49), channel_id=1, source_target_pairs={{0,19},{1,18},{2,17},{3,16},{4,23},{5,22},{6,21},{7,20},{8,27},{9,... | collective-permute-start | bytes 294920 | tf_op jit(solution)/shard_map/ppermute | solution.py:331
  106.0 12.2 %collective-permute-start.31 = (f32[192,128]{1,0:T(8,128)}, f32[192,128]{1,0:T(8,128)S(1)}, u32[]{:S(2)}, u32[]{:S(2)}) collective-permute-start(f32[192,128]{1,0:T(8,128)} %bitcast.48), channel_id=1, source_target_pairs={{0,20},{1,21},{2,22},{3,23},{4,16},{5,17},{6,18},{7,19},{8,28},{9,... | collective-permute-start | bytes 294920 | tf_op jit(solution)/shard_map/ppermute | solution.py:331
  113.3 7.5 %collective-permute-start.32 = (f32[192,128]{1,0:T(8,128)}, f32[192,128]{1,0:T(8,128)S(1)}, u32[]{:S(2)}, u32[]{:S(2)}) collective-permute-start(f32[192,128]{1,0:T(8,128)} %bitcast.47), channel_id=1, source_target_pairs={{0,21},{1,20},{2,23},{3,22},{4,17},{5,16},{6,19},{7,18},{8,29},{9,... | collective-permute-start | bytes 294920 | tf_op jit(solution)/shard_map/ppermute | solution.py:331
  115.4 23.8 %collective-permute-start.14 = (f32[192,128]{1,0:T(8,128)}, f32[192,128]{1,0:T(8,128)S(1)}, u32[]{:S(2)}, u32[]{:S(2)}) collective-permute-start(f32[192,128]{1,0:T(8,128)} %bitcast.46), channel_id=1, source_target_pairs={{0,28},{1,29},{2,30},{3,31},{4,24},{5,25},{6,26},{7,27},{8,20},{9,... | collective-permute-start | bytes 294920 | tf_op jit(solution)/shard_map/ppermute | solution.py:331
  118.1 21.1 %collective-permute-start.15 = (f32[192,128]{1,0:T(8,128)}, f32[192,128]{1,0:T(8,128)S(1)}, u32[]{:S(2)}, u32[]{:S(2)}) collective-permute-start(f32[192,128]{1,0:T(8,128)} %bitcast.45), channel_id=1, source_target_pairs={{0,29},{1,28},{2,31},{3,30},{4,25},{5,24},{6,27},{7,26},{8,21},{9,... | collective-permute-start | bytes 294920 | tf_op jit(solution)/shard_map/ppermute | solution.py:331
  120.8 18.4 %collective-permute-start.16 = (f32[192,128]{1,0:T(8,128)}, f32[192,128]{1,0:T(8,128)S(1)}, u32[]{:S(2)}, u32[]{:S(2)}) collective-permute-start(f32[192,128]{1,0:T(8,128)} %bitcast.44), channel_id=1, source_target_pairs={{0,30},{1,31},{2,28},{3,29},{4,26},{5,27},{6,24},{7,25},{8,22},{9,... | collective-permute-start | bytes 294920 | tf_op jit(solution)/shard_map/ppermute | solution.py:331
  123.3 15.9 %collective-permute-start.17 = (f32[192,128]{1,0:T(8,128)}, f32[192,128]{1,0:T(8,128)S(1)}, u32[]{:S(2)}, u32[]{:S(2)}) collective-permute-start(f32[192,128]{1,0:T(8,128)} %bitcast.43), channel_id=1, source_target_pairs={{0,31},{1,30},{2,29},{3,28},{4,27},{5,26},{6,25},{7,24},{8,23},{9,... | collective-permute-start | bytes 294920 | tf_op jit(solution)/shard_map/ppermute | solution.py:331
  (26 other events, 448.3 us)

commit v2 on v1

--- a/solution.py
+++ b/solution.py
@@ -268,8 +268,9 @@
             column = [ref[pl.ds(p * rows + i, k, stride=rows * parts), :] for ref, k in zip(refs, sizes)]
             columns.append(jnp.concatenate(column, axis=0))
     wh, wl = split(jnp.concatenate(columns, axis=1))
-    mh, ml = mh_ref[...], ml_ref[...]
-    out = mm(mh, wh) + mm(mh, wl) + mm(ml, wh)
+    mh = mh_ref[...]
+    both = mm(jnp.concatenate([mh, ml_ref[...]], axis=0), wh)
+    out = both[:mh.shape[0]] + both[mh.shape[0]:] + mm(mh, wl)
     o_ref[...] = out + refs[n + 2][...] if acc else out
 
 
@@ -371,8 +372,7 @@
         return general(me, runs_field, spectral_filter, block_inverses, factor_panels)
     rest = local - HEAD
     near = list(range(1, chips // 2))
-    mine = factor_panels[0]
-    mine = jnp.where(place < top, exchange(mine, top), mine)
+    mine = jnp.where(place < top, exchange(factor_panels, top)[0], factor_panels[0])
     (head,) = whiten(me, runs_field, spectral_filter, groups, 0, HEAD, HEAD, False)
     head = lax.all_to_all(head, "dev", 0, 0, tiled=True)
     outs = whiten(me, runs_field, spectral_filter, groups, HEAD, rest, HEAD, True)

time: 145 us -> 145 us (level)
  starting transfers between devices: 57.7 us -> 59.2 us
    ppermute x33, starting transfers between devices: 50.2 us -> 51.7 us  [exchange(): return lax.ppermute(x, 'dev', pairs)]
  transfers between devices with their start and end apart: 34 -> 34, of which waited for: 16 -> 18; matrix products, arithmetic and copies ran while one was open for 0% -> 0% of each run, Pallas kernels for 18% -> 18%
where the time goes in v2:
time: 145 us
  starting transfers between devices  59.2 us (41%)
  waiting for transfers between devices  47 us (32%)
  Pallas kernels  36.3 us (25%)
  local copies, waits for them, and re-layouts  2.25 us (2%)
    ppermute x33, starting transfers between devices, exchange(): return lax.ppermute(x, 'dev', pairs)  51.7 us
    ppermute x33, waiting for transfers between devices, exchange(): return lax.ppermute(x, 'dev', pairs)  47 us
    pallas_call x2, Pallas kernels, whiten(): pl.pallas_call(functools.partial(whiten_kernel, rb=rb, groups=groups, out...  16.1 us
    pallas_call x2, Pallas kernels, solve(): pl.pallas_call(functools.partial(solve_kernel, rows=rows, parts=parts, pe...  12.6 us
    all_to_all x1, starting transfers between devices, per_device(): head = lax.all_to_all(head, 'dev', 0, 0, tiled=True)  7.5 us
    pallas_call x1, Pallas kernels, mix(): pl.pallas_call(functools.partial(mix_kernel, top=top, local=local, stages...  3.92 us
  transfers between devices with their start and end apart: 34, of which 18 were waited for; matrix products, arithmetic and copies ran while one was open for 0% of the time, Pallas kernels for 18%

profile of v2, /device:TPU:0, one launch (start us, length us, event | category | flops | bytes accessed | tf_op | source)
XLA Modules:
  0.0 145.0 jit_solution(2869751022153381066)
XLA Ops:
  0.0 5.3 %whiten.3 = f32[32,4,2,8,128]{4,3,2,1,0:T(8,128)} custom-call(s32[1]{0:T(128)} %bitcast.me_ref, f32[16,256,256]{2,1,0:T(8,128)} %x_ref.3, f32[129,256]{1,0:T(8,128)} %bitcast.32, bf16[256,256]{1,0:T(8,128)(2,1)} %constant.30.clone.rest_0_, bf16[256,256]{1,0:T(8,128)(2,1)} %constant.31.clone.rest_1_, bf16[256,256]{1,0:T(8,128)(2,1)} %constant.32.clone.rest_2_, ...), custom_call_target="tpu_custom_call" | custom-call | tf_op jit(solution)/shard_map/whiten/pallas_call | solution.py:139
  5.3 7.5 %all-to-all-start = ((f32[32,4,2,8,128]{4,3,2,1,0:T(8,128)}), f32[32,4,2,8,128]{4,3,2,1,0:T(8,128)S(1)}, u32[]{:S(2)}, u32[]{:S(2)}) async-start(f32[32,4,2,8,128]{4,3,2,1,0:T(8,128)} %whiten.3), calls=%async_computation | async-start | bytes 2097152 | tf_op jit(solution)/shard_map/all_to_all | solution.py:377
  12.9 10.7 %whiten.2 = (f32[2,12,2,8,128]{4,3,2,1,0:T(8,128)}, f32[2,12,2,8,128]{4,3,2,1,0:T(8,128)}, f32[2,12,2,8,128]{4,3,2,1,0:T(8,128)}, f32[2,12,2,8,128]{4,3,2,1,0:T(...) custom-call(s32[1]{0:T(128)} %bitcast.me_ref, ...), custom_call_target="tpu_custom_call" | custom-call | tf_op jit(solution)/shard_map/whiten/pallas_call | solution.py:139
  23.6 1.7 %collective-permute-start = (f32[2,192,128]{2,1,0:T(8,128)}, f32[2,192,128]{2,1,0:T(8,128)S(1)}, u32[]{:S(2)}, u32[]{:S(2)}) collective-permute-start(f32[2,192,128]{2,1,0:T(8,128)} %bitcast.40), channel_id=1, source_target_pairs={{0,2},{1,3},{2,0},{3,1},{4,6},{5,7},{6,4},{7,5},{8,10},{9,11},{10,... | collective-permute-start | bytes 589832 | tf_op jit(solution)/shard_map/ppermute | solution.py:332
  30.2 2.8 %collective-permute-done.refs_1_.refs_2_ = f32[2,192,128]{2,1,0:T(8,128)S(1)} collective-permute-done((f32[2,192,128]{2,1,0:T(8,128)}, f32[2,192,128]{2,1,0:T(8,128)S(1)}, u32[]{:S(2)}, u32[]{:S(2)}) %collective-permute-start) | collective-permute-done | bytes 196640 | tf_op jit(solution)/shard_map/ppermute | solution.py:332
  33.0 2.9 %collective-permute-start.5 = (f32[2,192,128]{2,1,0:T(8,128)}, f32[2,192,128]{2,1,0:T(8,128)S(1)}, u32[]{:S(2)}, u32[]{:S(2)}) collective-permute-start(f32[2,192,128]{2,1,0:T(8,128)} %bitcast.35), channel_id=1, source_target_pairs={{0,12},{1,13},{2,14},{3,15},{4,8},{5,9},{6,10},{7,11},{8,4},{9,5},... | collective-permute-start | bytes 589832 | tf_op jit(solution)/shard_map/ppermute | solution.py:332
  35.9 2.8 %collective-permute-done.1.refs_2_.refs_3_ = f32[2,192,128]{2,1,0:T(8,128)S(1)} collective-permute-done((f32[2,192,128]{2,1,0:T(8,128)}, f32[2,192,128]{2,1,0:T(8,128)S(1)}, u32[]{:S(2)}, u32[]{:S(2)}) %collective-permute-start.1) | collective-permute-done | bytes 196640 | tf_op jit(solution)/shard_map/ppermute | solution.py:332
  39.9 4.4 %collective-permute-done.4.refs_5_.refs_1_ = f32[2,192,128]{2,1,0:T(8,128)S(1)} collective-permute-done((f32[2,192,128]{2,1,0:T(8,128)}, f32[2,192,128]{2,1,0:T(8,128)S(1)}, u32[]{:S(2)}, u32[]{:S(2)}) %collective-permute-start.4) | collective-permute-done | bytes 196640 | tf_op jit(solution)/shard_map/ppermute | solution.py:332
  44.3 4.1 %collective-permute-done.5.refs_6_.refs_2_ = f32[2,192,128]{2,1,0:T(8,128)S(1)} collective-permute-done((f32[2,192,128]{2,1,0:T(8,128)}, f32[2,192,128]{2,1,0:T(8,128)S(1)}, u32[]{:S(2)}, u32[]{:S(2)}) %collective-permute-start.5) | collective-permute-done | bytes 196640 | tf_op jit(solution)/shard_map/ppermute | solution.py:332
  48.4 4.6 %collective-permute-done.6.refs_7_.refs_3_ = f32[2,192,128]{2,1,0:T(8,128)S(1)} collective-permute-done((f32[2,192,128]{2,1,0:T(8,128)}, f32[2,192,128]{2,1,0:T(8,128)S(1)}, u32[]{:S(2)}, u32[]{:S(2)}) %collective-permute-start.6) | collective-permute-done | bytes 196640 | tf_op jit(solution)/shard_map/ppermute | solution.py:332
  53.7 2.2 %bundle.1 = f32[1536,128]{1,0:T(8,128)} custom-call(s32[1]{0:T(128)} %bitcast.me_ref, f32[2,192,128]{2,1,0:T(8,128)} %bitcast.30, f32[2,192,128]{2,1,0:T(8,128)} %copy-done.4, f32[2,192,128]{2,1,0:T(8,128)} %copy-done.5, f32[2,192,128]{2,1,0:T(8,128)} %copy-done.6, f32[2,192,128]{2,1,0:T(8,128)} %copy-done.7, f32[2,192,128]{2,1,0:T(8,128)} %copy-done.1, ...), custom_call_target="tpu_custom_call" | custom-call | tf_op jit(solution)/shard_map/bundle/pallas_call | solution.py:197
  55.9 1.9 %collective-permute-start.18 = (f32[2,16,256]{2,1,0:T(8,128)S(1)}, f32[2,16,256]{2,1,0:T(8,128)S(1)}, u32[]{:S(2)}, u32[]{:S(2)}) collective-permute-start(f32[2,16,256]{2,1,0:T(8,128)S(1)} %copy-done.23), channel_id=1, source_target_pairs={{0,16},{1,17},{2,18},{3,19},{4,20},{5,21},{6,22},{7,23},{8,24},{9,... | collective-permute-start | bytes 98312 | tf_op jit(solution)/shard_map/ppermute | solution.py:332
  58.5 2.8 %collective-permute-done.18 = f32[2,16,256]{2,1,0:T(8,128)S(1)} collective-permute-done((f32[2,16,256]{2,1,0:T(8,128)S(1)}, f32[2,16,256]{2,1,0:T(8,128)S(1)}, u32[]{:S(2)}, u32[]{:S(2)}) %collective-permute-start.18) | collective-permute-done | bytes 32800 | tf_op jit(solution)/shard_map/ppermute | solution.py:332
  61.8 2.4 %collective-permute-start.24 = (f32[16,256]{1,0:T(8,128)S(1)}, f32[16,256]{1,0:T(8,128)S(1)}, u32[]{:S(2)}, u32[]{:S(2)}) collective-permute-start(f32[16,256]{1,0:T(8,128)S(1)} %fusion.refs_0_.refs_5_), channel_id=1, source_target_pairs={{0,12},{1,13},{2,14},{3,15},{4,8},{5,9},{6,10},{7,11},{8,4},{9,5},... | collective-permute-start | bytes 49160 | tf_op jit(solution)/shard_map/ppermute | solution.py:332
  65.2 3.0 %collective-permute-done.25.refs_7_.refs_12_ = f32[16,256]{1,0:T(8,128)S(1)} collective-permute-done((f32[16,256]{1,0:T(8,128)S(1)}, f32[16,256]{1,0:T(8,128)S(1)}, u32[]{:S(2)}, u32[]{:S(2)}) %collective-permute-start.25) | collective-permute-done | bytes 16416 | tf_op jit(solution)/shard_map/ppermute | solution.py:332
  68.8 3.0 %collective-permute-done.22.refs_4_.refs_9_ = f32[16,256]{1,0:T(8,128)S(1)} collective-permute-done((f32[16,256]{1,0:T(8,128)S(1)}, f32[16,256]{1,0:T(8,128)S(1)}, u32[]{:S(2)}, u32[]{:S(2)}) %collective-permute-start.22) | collective-permute-done | bytes 16416 | tf_op jit(solution)/shard_map/ppermute | solution.py:332
  73.6 2.2 %collective-permute-done.20.refs_2_.refs_7_ = f32[16,256]{1,0:T(8,128)S(1)} collective-permute-done((f32[16,256]{1,0:T(8,128)S(1)}, f32[16,256]{1,0:T(8,128)S(1)}, u32[]{:S(2)}, u32[]{:S(2)}) %collective-permute-start.20) | collective-permute-done | bytes 16416 | tf_op jit(solution)/shard_map/ppermute | solution.py:332
  75.8 2.5 %collective-permute-start.10 = (f32[192,128]{1,0:T(8,128)}, f32[192,128]{1,0:T(8,128)S(1)}, u32[]{:S(2)}, u32[]{:S(2)}) collective-permute-start(f32[192,128]{1,0:T(8,128)} %bitcast.54), channel_id=1, source_target_pairs={{0,24},{1,25},{2,26},{3,27},{4,28},{5,29},{6,30},{7,31},{8,16},{9,... | collective-permute-start | bytes 294920 | tf_op jit(solution)/shard_map/ppermute | solution.py:332
  79.0 3.0 %collective-permute-start.12 = (f32[192,128]{1,0:T(8,128)}, f32[192,128]{1,0:T(8,128)S(1)}, u32[]{:S(2)}, u32[]{:S(2)}) collective-permute-start(f32[192,128]{1,0:T(8,128)} %bitcast.52), channel_id=1, source_target_pairs={{0,26},{1,27},{2,24},{3,25},{4,30},{5,31},{6,28},{7,29},{8,18},{9,... | collective-permute-start | bytes 294920 | tf_op jit(solution)/shard_map/ppermute | solution.py:332
  82.0 1.8 %collective-permute-start.13 = (f32[192,128]{1,0:T(8,128)}, f32[192,128]{1,0:T(8,128)S(1)}, u32[]{:S(2)}, u32[]{:S(2)}) collective-permute-start(f32[192,128]{1,0:T(8,128)} %bitcast.51), channel_id=1, source_target_pairs={{0,27},{1,26},{2,25},{3,24},{4,31},{5,30},{6,29},{7,28},{8,19},{9,... | collective-permute-start | bytes 294920 | tf_op jit(solution)/shard_map/ppermute | solution.py:332
  85.4 8.7 %collective-permute-start.28 = (f32[192,128]{1,0:T(8,128)}, f32[192,128]{1,0:T(8,128)S(1)}, u32[]{:S(2)}, u32[]{:S(2)}) collective-permute-start(f32[192,128]{1,0:T(8,128)} %bitcast.49), channel_id=1, source_target_pairs={{0,17},{1,16},{2,19},{3,18},{4,21},{5,20},{6,23},{7,22},{8,25},{9,... | collective-permute-start | bytes 294920 | tf_op jit(solution)/shard_map/ppermute | solution.py:332
  94.1 3.6 %collective-permute-start.29 = (f32[192,128]{1,0:T(8,128)}, f32[192,128]{1,0:T(8,128)S(1)}, u32[]{:S(2)}, u32[]{:S(2)}) collective-permute-start(f32[192,128]{1,0:T(8,128)} %bitcast.48), channel_id=1, source_target_pairs={{0,18},{1,19},{2,16},{3,17},{4,22},{5,23},{6,20},{7,21},{8,26},{9,... | collective-permute-start | bytes 294920 | tf_op jit(solution)/shard_map/ppermute | solution.py:332
  99.3 4.8 %collective-permute-done.27.refs_6_ = f32[192,128]{1,0:T(8,128)S(1)} collective-permute-done((f32[192,128]{1,0:T(8,128)}, f32[192,128]{1,0:T(8,128)S(1)}, u32[]{:S(2)}, u32[]{:S(2)}) %collective-permute-start.27) | collective-permute-done | bytes 98336 | tf_op jit(solution)/shard_map/ppermute | solution.py:332
  104.1 1.7 %collective-permute-done.28.refs_7_ = f32[192,128]{1,0:T(8,128)S(1)} collective-permute-done((f32[192,128]{1,0:T(8,128)}, f32[192,128]{1,0:T(8,128)S(1)}, u32[]{:S(2)}, u32[]{:S(2)}) %collective-permute-start.28) | collective-permute-done | bytes 98336 | tf_op jit(solution)/shard_map/ppermute | solution.py:332
  109.5 5.8 %collective-permute-done.30.refs_9_ = f32[192,128]{1,0:T(8,128)S(1)} collective-permute-done((f32[192,128]{1,0:T(8,128)}, f32[192,128]{1,0:T(8,128)S(1)}, u32[]{:S(2)}, u32[]{:S(2)}) %collective-permute-start.30) | collective-permute-done | bytes 98336 | tf_op jit(solution)/shard_map/ppermute | solution.py:332
  115.3 3.4 %collective-permute-start.14 = (f32[192,128]{1,0:T(8,128)}, f32[192,128]{1,0:T(8,128)S(1)}, u32[]{:S(2)}, u32[]{:S(2)}) collective-permute-start(f32[192,128]{1,0:T(8,128)} %bitcast.44), channel_id=1, source_target_pairs={{0,28},{1,29},{2,30},{3,31},{4,24},{5,25},{6,26},{7,27},{8,20},{9,... | collective-permute-start | bytes 294920 | tf_op jit(solution)/shard_map/ppermute | solution.py:332
  118.9 2.0 %collective-permute-start.15 = (f32[192,128]{1,0:T(8,128)}, f32[192,128]{1,0:T(8,128)S(1)}, u32[]{:S(2)}, u32[]{:S(2)}) collective-permute-start(f32[192,128]{1,0:T(8,128)} %bitcast.43), channel_id=1, source_target_pairs={{0,29},{1,28},{2,31},{3,30},{4,25},{5,24},{6,27},{7,26},{8,21},{9,... | collective-permute-start | bytes 294920 | tf_op jit(solution)/shard_map/ppermute | solution.py:332
  120.8 2.8 %collective-permute-start.16 = (f32[192,128]{1,0:T(8,128)}, f32[192,128]{1,0:T(8,128)S(1)}, u32[]{:S(2)}, u32[]{:S(2)}) collective-permute-start(f32[192,128]{1,0:T(8,128)} %bitcast.42), channel_id=1, source_target_pairs={{0,30},{1,31},{2,28},{3,29},{4,26},{5,27},{6,24},{7,25},{8,22},{9,... | collective-permute-start | bytes 294920 | tf_op jit(solution)/shard_map/ppermute | solution.py:332
  123.6 3.3 %collective-permute-start.17 = (f32[192,128]{1,0:T(8,128)}, f32[192,128]{1,0:T(8,128)S(1)}, u32[]{:S(2)}, u32[]{:S(2)}) collective-permute-start(f32[192,128]{1,0:T(8,128)} %bitcast.41), channel_id=1, source_target_pairs={{0,31},{1,30},{2,29},{3,28},{4,27},{5,26},{6,25},{7,24},{8,23},{9,... | collective-permute-start | bytes 294920 | tf_op jit(solution)/shard_map/ppermute | solution.py:332
  127.5 3.9 %mix.1 = (bf16[512,260]{1,0:T(8,128)(2,1)}, bf16[512,260]{1,0:T(8,128)(2,1)}, bf16[512,252]{1,0:T(8,128)(2,1)}, bf16[512,252]{1,0:T(8,128)(2,1)}) custom-call(s32[1]{0:T(128)} %bitcast.me_ref, s32[1,260]{1,0:T(1,128)} %constant.38.clone.refs_0_, s32[1,260]{1,0:T(1,128)} %constant.39.clone.refs_1_, s32[1,252]{1,0:T(1,128)} %constant.40.clone.refs_2_, ...), custom_call_target="tpu_custom_call" | custom-call | tf_op jit(solution)/shard_map/mix/pallas_call | solution.py:248
  132.4 7.1 %solve.2.refs_16_ = f32[512,2048]{1,0:T(8,128)} custom-call(s32[1]{0:T(128)} %bitcast.me_ref, f32[2048,128]{1,0:T(8,128)} %bitcast.29, f32[2,192,128]{2,1,0:T(8,128)} %bitcast.31, f32[2,192,128]{2,1,0:T(8,128)} %copy-done.4, f32[2,192,128]{2,1,0:T(8,128)} %copy-done.5, f32[2,192,128]{2,1,0:T(8,128)} %copy-done.6, f32[2,192,128]{2,1,0:T(8,128)} %copy-done.7, ...), custom_call_target="tpu_custom_call" | custom-call | tf_op jit(solution)/shard_map/solve/pallas_call | solution.py:288
  139.6 5.5 %solve.3 = f32[512,2048]{1,0:T(8,128)} custom-call(s32[1]{0:T(128)} %bitcast.me_ref, f32[1536,128]{1,0:T(8,128)S(1)} %collective-permute-done.7.refs_0_, f32[2,192,128]{2,1,0:T(8,128)} %copy-done.1, f32[2,192,128]{2,1,0:T(8,128)} %copy-done.2, f32[2,192,128]{2,1,0:T(8,128)} %copy-done.3, ...), custom_call_target="tpu_custom_call", output_to_operand_aliasing={{}: (17, {})} | custom-call | tf_op jit(solution)/shard_map/solve/pallas_call | solution.py:288
  (93 shorter events, 20.6 us)
Async XLA Ops:
  5.3 126.0 %all-to-all-start = ((f32[32,4,2,8,128]{4,3,2,1,0:T(8,128)}), f32[32,4,2,8,128]{4,3,2,1,0:T(8,128)S(1)}, u32[]{:S(2)}, u32[]{:S(2)}) async-start(f32[32,4,2,8,128]{4,3,2,1,0:T(8,128)} %whiten.3), calls=%async_computation | async-start | bytes 2097152 | tf_op jit(solution)/shard_map/all_to_all | solution.py:377
  23.6 9.4 %collective-permute-start = (f32[2,192,128]{2,1,0:T(8,128)}, f32[2,192,128]{2,1,0:T(8,128)S(1)}, u32[]{:S(2)}, u32[]{:S(2)}) collective-permute-start(f32[2,192,128]{2,1,0:T(8,128)} %bitcast.40), channel_id=1, source_target_pairs={{0,2},{1,3},{2,0},{3,1},{4,6},{5,7},{6,4},{7,5},{8,10},{9,11},{10,... | collective-permute-start | bytes 589832 | tf_op jit(solution)/shard_map/ppermute | solution.py:332
  25.3 13.5 %collective-permute-start.1 = (f32[2,192,128]{2,1,0:T(8,128)}, f32[2,192,128]{2,1,0:T(8,128)S(1)}, u32[]{:S(2)}, u32[]{:S(2)}) collective-permute-start(f32[2,192,128]{2,1,0:T(8,128)} %bitcast.39), channel_id=1, source_target_pairs={{0,4},{1,5},{2,6},{3,7},{4,0},{5,1},{6,2},{7,3},{8,12},{9,13},{10,... | collective-permute-start | bytes 589832 | tf_op jit(solution)/shard_map/ppermute | solution.py:332
  26.7 13.1 %collective-permute-start.2 = (f32[2,192,128]{2,1,0:T(8,128)}, f32[2,192,128]{2,1,0:T(8,128)S(1)}, u32[]{:S(2)}, u32[]{:S(2)}) collective-permute-start(f32[2,192,128]{2,1,0:T(8,128)} %bitcast.38), channel_id=1, source_target_pairs={{0,6},{1,7},{2,4},{3,5},{4,2},{5,3},{6,0},{7,1},{8,14},{9,15},{10,... | collective-permute-start | bytes 589832 | tf_op jit(solution)/shard_map/ppermute | solution.py:332
  27.2 12.7 %collective-permute-start.3 = (f32[2,192,128]{2,1,0:T(8,128)}, f32[2,192,128]{2,1,0:T(8,128)S(1)}, u32[]{:S(2)}, u32[]{:S(2)}) collective-permute-start(f32[2,192,128]{2,1,0:T(8,128)} %bitcast.37), channel_id=1, source_target_pairs={{0,8},{1,9},{2,10},{3,11},{4,12},{5,13},{6,14},{7,15},{8,0},{9,1},... | collective-permute-start | bytes 589832 | tf_op jit(solution)/shard_map/ppermute | solution.py:332
  28.8 15.5 %collective-permute-start.4 = (f32[2,192,128]{2,1,0:T(8,128)}, f32[2,192,128]{2,1,0:T(8,128)S(1)}, u32[]{:S(2)}, u32[]{:S(2)}) collective-permute-start(f32[2,192,128]{2,1,0:T(8,128)} %bitcast.36), channel_id=1, source_target_pairs={{0,10},{1,11},{2,8},{3,9},{4,14},{5,15},{6,12},{7,13},{8,2},{9,3},... | collective-permute-start | bytes 589832 | tf_op jit(solution)/shard_map/ppermute | solution.py:332
  33.0 15.4 %collective-permute-start.5 = (f32[2,192,128]{2,1,0:T(8,128)}, f32[2,192,128]{2,1,0:T(8,128)S(1)}, u32[]{:S(2)}, u32[]{:S(2)}) collective-permute-start(f32[2,192,128]{2,1,0:T(8,128)} %bitcast.35), channel_id=1, source_target_pairs={{0,12},{1,13},{2,14},{3,15},{4,8},{5,9},{6,10},{7,11},{8,4},{9,5},... | collective-permute-start | bytes 589832 | tf_op jit(solution)/shard_map/ppermute | solution.py:332
  38.8 14.2 %collective-permute-start.6 = (f32[2,192,128]{2,1,0:T(8,128)}, f32[2,192,128]{2,1,0:T(8,128)S(1)}, u32[]{:S(2)}, u32[]{:S(2)}) collective-permute-start(f32[2,192,128]{2,1,0:T(8,128)} %bitcast.34), channel_id=1, source_target_pairs={{0,14},{1,15},{2,12},{3,13},{4,10},{5,11},{6,8},{7,9},{8,6},{9,7},... | collective-permute-start | bytes 589832 | tf_op jit(solution)/shard_map/ppermute | solution.py:332
  55.9 83.7 %collective-permute-start.7 = (f32[1536,128]{1,0:T(8,128)}, f32[1536,128]{1,0:T(8,128)S(1)}, u32[]{:S(2)}, u32[]{:S(2)}) collective-permute-start(f32[1536,128]{1,0:T(8,128)} %bundle.1), channel_id=1, source_target_pairs={{0,1},{1,0},{2,3},{3,2},{4,5},{5,4},{6,7},{7,6},{8,9},{9,8},{10,11... | collective-permute-start | bytes 2359304 | tf_op jit(solution)/shard_map/ppermute | solution.py:332
  55.9 5.4 %collective-permute-start.18 = (f32[2,16,256]{2,1,0:T(8,128)S(1)}, f32[2,16,256]{2,1,0:T(8,128)S(1)}, u32[]{:S(2)}, u32[]{:S(2)}) collective-permute-start(f32[2,16,256]{2,1,0:T(8,128)S(1)} %copy-done.23), channel_id=1, source_target_pairs={{0,16},{1,17},{2,18},{3,19},{4,20},{5,21},{6,22},{7,23},{8,24},{9,... | collective-permute-start | bytes 98312 | tf_op jit(solution)/shard_map/ppermute | solution.py:332
  57.7 21.3 %collective-permute-start.8 = (f32[192,128]{1,0:T(8,128)}, f32[192,128]{1,0:T(8,128)S(1)}, u32[]{:S(2)}, u32[]{:S(2)}) collective-permute-start(f32[192,128]{1,0:T(8,128)} %bitcast.56), channel_id=1, source_target_pairs={{0,22},{1,23},{2,20},{3,21},{4,18},{5,19},{6,16},{7,17},{8,30},{9,... | collective-permute-start | bytes 294920 | tf_op jit(solution)/shard_map/ppermute | solution.py:332
  61.3 6.9 %collective-permute-start.25 = (f32[16,256]{1,0:T(8,128)S(1)}, f32[16,256]{1,0:T(8,128)S(1)}, u32[]{:S(2)}, u32[]{:S(2)}) collective-permute-start(f32[16,256]{1,0:T(8,128)S(1)} %fusion.refs_0_.refs_5_), channel_id=1, source_target_pairs={{0,14},{1,15},{2,12},{3,13},{4,10},{5,11},{6,8},{7,9},{8,6},{9,7},... | collective-permute-start | bytes 49160 | tf_op jit(solution)/shard_map/ppermute | solution.py:332
  61.8 6.4 %collective-permute-start.24 = (f32[16,256]{1,0:T(8,128)S(1)}, f32[16,256]{1,0:T(8,128)S(1)}, u32[]{:S(2)}, u32[]{:S(2)}) collective-permute-start(f32[16,256]{1,0:T(8,128)S(1)} %fusion.refs_0_.refs_5_), channel_id=1, source_target_pairs={{0,12},{1,13},{2,14},{3,15},{4,8},{5,9},{6,10},{7,11},{8,4},{9,5},... | collective-permute-start | bytes 49160 | tf_op jit(solution)/shard_map/ppermute | solution.py:332
  64.2 4.6 %collective-permute-start.23 = (f32[16,256]{1,0:T(8,128)S(1)}, f32[16,256]{1,0:T(8,128)S(1)}, u32[]{:S(2)}, u32[]{:S(2)}) collective-permute-start(f32[16,256]{1,0:T(8,128)S(1)} %fusion.refs_0_.refs_5_), channel_id=1, source_target_pairs={{0,10},{1,11},{2,8},{3,9},{4,14},{5,15},{6,12},{7,13},{8,2},{9,3},... | collective-permute-start | bytes 49160 | tf_op jit(solution)/shard_map/ppermute | solution.py:332
  68.1 4.7 %collective-permute-start.21 = (f32[16,256]{1,0:T(8,128)S(1)}, f32[16,256]{1,0:T(8,128)S(1)}, u32[]{:S(2)}, u32[]{:S(2)}) collective-permute-start(f32[16,256]{1,0:T(8,128)S(1)} %fusion.refs_0_.refs_5_), channel_id=1, source_target_pairs={{0,6},{1,7},{2,4},{3,5},{4,2},{5,3},{6,0},{7,1},{8,14},{9,15},{10,... | collective-permute-start | bytes 49160 | tf_op jit(solution)/shard_map/ppermute | solution.py:332
  68.8 13.2 %collective-permute-start.9 = (f32[192,128]{1,0:T(8,128)}, f32[192,128]{1,0:T(8,128)S(1)}, u32[]{:S(2)}, u32[]{:S(2)}) collective-permute-start(f32[192,128]{1,0:T(8,128)} %bitcast.55), channel_id=1, source_target_pairs={{0,23},{1,22},{2,21},{3,20},{4,19},{5,18},{6,17},{7,16},{8,31},{9,... | collective-permute-start | bytes 294920 | tf_op jit(solution)/shard_map/ppermute | solution.py:332
  72.9 5.4 %collective-permute-start.19 = (f32[16,256]{1,0:T(8,128)S(1)}, f32[16,256]{1,0:T(8,128)S(1)}, u32[]{:S(2)}, u32[]{:S(2)}) collective-permute-start(f32[16,256]{1,0:T(8,128)S(1)} %fusion.refs_0_.refs_5_), channel_id=1, source_target_pairs={{0,2},{1,3},{2,0},{3,1},{4,6},{5,7},{6,4},{7,5},{8,10},{9,11},{10,... | collective-permute-start | bytes 49160 | tf_op jit(solution)/shard_map/ppermute | solution.py:332
  75.8 8.0 %collective-permute-start.10 = (f32[192,128]{1,0:T(8,128)}, f32[192,128]{1,0:T(8,128)S(1)}, u32[]{:S(2)}, u32[]{:S(2)}) collective-permute-start(f32[192,128]{1,0:T(8,128)} %bitcast.54), channel_id=1, source_target_pairs={{0,24},{1,25},{2,26},{3,27},{4,28},{5,29},{6,30},{7,31},{8,16},{9,... | collective-permute-start | bytes 294920 | tf_op jit(solution)/shard_map/ppermute | solution.py:332
  78.3 7.2 %collective-permute-start.11 = (f32[192,128]{1,0:T(8,128)}, f32[192,128]{1,0:T(8,128)S(1)}, u32[]{:S(2)}, u32[]{:S(2)}) collective-permute-start(f32[192,128]{1,0:T(8,128)} %bitcast.53), channel_id=1, source_target_pairs={{0,25},{1,24},{2,27},{3,26},{4,29},{5,28},{6,31},{7,30},{8,17},{9,... | collective-permute-start | bytes 294920 | tf_op jit(solution)/shard_map/ppermute | solution.py:332
  79.0 15.1 %collective-permute-start.12 = (f32[192,128]{1,0:T(8,128)}, f32[192,128]{1,0:T(8,128)S(1)}, u32[]{:S(2)}, u32[]{:S(2)}) collective-permute-start(f32[192,128]{1,0:T(8,128)} %bitcast.52), channel_id=1, source_target_pairs={{0,26},{1,27},{2,24},{3,25},{4,30},{5,31},{6,28},{7,29},{8,18},{9,... | collective-permute-start | bytes 294920 | tf_op jit(solution)/shard_map/ppermute | solution.py:332
  82.0 17.3 %collective-permute-start.13 = (f32[192,128]{1,0:T(8,128)}, f32[192,128]{1,0:T(8,128)S(1)}, u32[]{:S(2)}, u32[]{:S(2)}) collective-permute-start(f32[192,128]{1,0:T(8,128)} %bitcast.51), channel_id=1, source_target_pairs={{0,27},{1,26},{2,25},{3,24},{4,31},{5,30},{6,29},{7,28},{8,19},{9,... | collective-permute-start | bytes 294920 | tf_op jit(solution)/shard_map/ppermute | solution.py:332
  83.8 20.3 %collective-permute-start.27 = (f32[192,128]{1,0:T(8,128)}, f32[192,128]{1,0:T(8,128)S(1)}, u32[]{:S(2)}, u32[]{:S(2)}) collective-permute-start(f32[192,128]{1,0:T(8,128)} %bitcast.50), channel_id=1, source_target_pairs={{0,16},{1,17},{2,18},{3,19},{4,20},{5,21},{6,22},{7,23},{8,24},{9,... | collective-permute-start | bytes 294920 | tf_op jit(solution)/shard_map/ppermute | solution.py:332
  85.4 20.4 %collective-permute-start.28 = (f32[192,128]{1,0:T(8,128)}, f32[192,128]{1,0:T(8,128)S(1)}, u32[]{:S(2)}, u32[]{:S(2)}) collective-permute-start(f32[192,128]{1,0:T(8,128)} %bitcast.49), channel_id=1, source_target_pairs={{0,17},{1,16},{2,19},{3,18},{4,21},{5,20},{6,23},{7,22},{8,25},{9,... | collective-permute-start | bytes 294920 | tf_op jit(solution)/shard_map/ppermute | solution.py:332
  94.1 13.8 %collective-permute-start.29 = (f32[192,128]{1,0:T(8,128)}, f32[192,128]{1,0:T(8,128)S(1)}, u32[]{:S(2)}, u32[]{:S(2)}) collective-permute-start(f32[192,128]{1,0:T(8,128)} %bitcast.48), channel_id=1, source_target_pairs={{0,18},{1,19},{2,16},{3,17},{4,22},{5,23},{6,20},{7,21},{8,26},{9,... | collective-permute-start | bytes 294920 | tf_op jit(solution)/shard_map/ppermute | solution.py:332
  99.3 24.3 %collective-permute-start.26 = (f32[128,256]{1,0:T(8,128)}, f32[128,256]{1,0:T(8,128)S(1)}, u32[]{:S(2)}, u32[]{:S(2)}) collective-permute-start(f32[128,256]{1,0:T(8,128)} %stack.1), channel_id=1, source_target_pairs={{0,1},{1,0},{2,3},{3,2},{4,5},{5,4},{6,7},{7,6},{8,9},{9,8},{10,11... | collective-permute-start | bytes 393224 | tf_op jit(solution)/shard_map/ppermute | solution.py:332
  104.1 11.2 %collective-permute-start.30 = (f32[192,128]{1,0:T(8,128)}, f32[192,128]{1,0:T(8,128)S(1)}, u32[]{:S(2)}, u32[]{:S(2)}) collective-permute-start(f32[192,128]{1,0:T(8,128)} %bitcast.47), channel_id=1, source_target_pairs={{0,19},{1,18},{2,17},{3,16},{4,23},{5,22},{6,21},{7,20},{8,27},{9,... | collective-permute-start | bytes 294920 | tf_op jit(solution)/shard_map/ppermute | solution.py:332
  105.8 13.0 %collective-permute-start.31 = (f32[192,128]{1,0:T(8,128)}, f32[192,128]{1,0:T(8,128)S(1)}, u32[]{:S(2)}, u32[]{:S(2)}) collective-permute-start(f32[192,128]{1,0:T(8,128)} %bitcast.46), channel_id=1, source_target_pairs={{0,20},{1,21},{2,22},{3,23},{4,16},{5,17},{6,18},{7,19},{8,28},{9,... | collective-permute-start | bytes 294920 | tf_op jit(solution)/shard_map/ppermute | solution.py:332
  108.0 12.9 %collective-permute-start.32 = (f32[192,128]{1,0:T(8,128)}, f32[192,128]{1,0:T(8,128)S(1)}, u32[]{:S(2)}, u32[]{:S(2)}) collective-permute-start(f32[192,128]{1,0:T(8,128)} %bitcast.45), channel_id=1, source_target_pairs={{0,21},{1,20},{2,23},{3,22},{4,17},{5,16},{6,19},{7,18},{8,29},{9,... | collective-permute-start | bytes 294920 | tf_op jit(solution)/shard_map/ppermute | solution.py:332
  115.3 24.2 %collective-permute-start.14 = (f32[192,128]{1,0:T(8,128)}, f32[192,128]{1,0:T(8,128)S(1)}, u32[]{:S(2)}, u32[]{:S(2)}) collective-permute-start(f32[192,128]{1,0:T(8,128)} %bitcast.44), channel_id=1, source_target_pairs={{0,28},{1,29},{2,30},{3,31},{4,24},{5,25},{6,26},{7,27},{8,20},{9,... | collective-permute-start | bytes 294920 | tf_op jit(solution)/shard_map/ppermute | solution.py:332
  118.9 20.7 %collective-permute-start.15 = (f32[192,128]{1,0:T(8,128)}, f32[192,128]{1,0:T(8,128)S(1)}, u32[]{:S(2)}, u32[]{:S(2)}) collective-permute-start(f32[192,128]{1,0:T(8,128)} %bitcast.43), channel_id=1, source_target_pairs={{0,29},{1,28},{2,31},{3,30},{4,25},{5,24},{6,27},{7,26},{8,21},{9,... | collective-permute-start | bytes 294920 | tf_op jit(solution)/shard_map/ppermute | solution.py:332
  120.8 18.7 %collective-permute-start.16 = (f32[192,128]{1,0:T(8,128)}, f32[192,128]{1,0:T(8,128)S(1)}, u32[]{:S(2)}, u32[]{:S(2)}) collective-permute-start(f32[192,128]{1,0:T(8,128)} %bitcast.42), channel_id=1, source_target_pairs={{0,30},{1,31},{2,28},{3,29},{4,26},{5,27},{6,24},{7,25},{8,22},{9,... | collective-permute-start | bytes 294920 | tf_op jit(solution)/shard_map/ppermute | solution.py:332
  123.6 15.9 %collective-permute-start.17 = (f32[192,128]{1,0:T(8,128)}, f32[192,128]{1,0:T(8,128)S(1)}, u32[]{:S(2)}, u32[]{:S(2)}) collective-permute-start(f32[192,128]{1,0:T(8,128)} %bitcast.41), channel_id=1, source_target_pairs={{0,31},{1,30},{2,29},{3,28},{4,27},{5,26},{6,25},{7,24},{8,23},{9,... | collective-permute-start | bytes 294920 | tf_op jit(solution)/shard_map/ppermute | solution.py:332
  (26 other events, 462.6 us)

commit v3 on v1

--- a/solution.py
+++ b/solution.py
@@ -66,8 +66,8 @@
     diffs = (jnp.where(edge, 0.0, plus) - minus).astype(jnp.bfloat16)
     table = exact_pick(plus[:, :half].astype(jnp.bfloat16), filter_t[:half], ((1,), (0,)))
     table = jnp.where(freq == half, jnp.broadcast_to(filter_t[half:half + 1], table.shape), table)
-    s = exact_pick(sums, table, ((1,), (1,)))
-    d = exact_pick(diffs, table, ((1,), (1,)))
+    both = exact_pick(jnp.concatenate([sums, diffs], axis=0), table, ((1,), (1,)))
+    s, d = both[:length], both[length:]
     across, other = frequency(col, length)
     border = (across == 0) | (across == half)
     scale = 1.0 / float(length * length)
@@ -371,8 +371,7 @@
         return general(me, runs_field, spectral_filter, block_inverses, factor_panels)
     rest = local - HEAD
     near = list(range(1, chips // 2))
-    mine = factor_panels[0]
-    mine = jnp.where(place < top, exchange(mine, top), mine)
+    mine = jnp.where(place < top, exchange(factor_panels, top)[0], factor_panels[0])
     (head,) = whiten(me, runs_field, spectral_filter, groups, 0, HEAD, HEAD, False)
     head = lax.all_to_all(head, "dev", 0, 0, tiled=True)
     outs = whiten(me, runs_field, spectral_filter, groups, HEAD, rest, HEAD, True)

time: 145 us -> 146 us (level)
  transfers between devices with their start and end apart: 34 -> 34, of which waited for: 16 -> 17; matrix products, arithmetic and copies ran while one was open for 0% -> 0% of each run, Pallas kernels for 18% -> 18%
where the time goes in v3:
time: 146 us; the launch traced here: 145 us
  starting transfers between devices  57.8 us (40%)
  waiting for transfers between devices  48.4 us (33%)
  Pallas kernels  36.5 us (25%)
  local copies, waits for them, and re-layouts  2.25 us (2%)
    ppermute x33, starting transfers between devices, exchange(): return lax.ppermute(x, 'dev', pairs)  50.3 us
    ppermute x33, waiting for transfers between devices, exchange(): return lax.ppermute(x, 'dev', pairs)  48.4 us
    pallas_call x2, Pallas kernels, whiten(): pl.pallas_call(functools.partial(whiten_kernel, rb=rb, groups=groups, out...  16.3 us
    pallas_call x2, Pallas kernels, solve(): pl.pallas_call(functools.partial(solve_kernel, rows=rows, parts=parts, pe...  12.6 us
    all_to_all x1, starting transfers between devices, per_device(): head = lax.all_to_all(head, 'dev', 0, 0, tiled=True)  7.51 us
    pallas_call x1, Pallas kernels, mix(): pl.pallas_call(functools.partial(mix_kernel, top=top, local=local, stages...  3.92 us
  transfers between devices with their start and end apart: 34, of which 17 were waited for; matrix products, arithmetic and copies ran while one was open for 0% of the time, Pallas kernels for 18%

profile of v3, /device:TPU:0, one launch (start us, length us, event | category | flops | bytes accessed | tf_op | source)
XLA Modules:
  0.0 145.2 jit_solution(1210509056172103612)
XLA Ops:
  0.0 5.5 %whiten.3 = f32[32,4,2,8,128]{4,3,2,1,0:T(8,128)} custom-call(s32[1]{0:T(128)} %bitcast.me_ref, f32[16,256,256]{2,1,0:T(8,128)} %x_ref.3, f32[129,256]{1,0:T(8,128)} %bitcast.32, bf16[256,256]{1,0:T(8,128)(2,1)} %constant.30.clone.rest_0_, bf16[256,256]{1,0:T(8,128)(2,1)} %constant.31.clone.rest_1_, bf16[256,256]{1,0:T(8,128)(2,1)} %constant.32.clone.rest_2_, ...), custom_call_target="tpu_custom_call" | custom-call | tf_op jit(solution)/shard_map/whiten/pallas_call | solution.py:139
  5.5 7.5 %all-to-all-start = ((f32[32,4,2,8,128]{4,3,2,1,0:T(8,128)}), f32[32,4,2,8,128]{4,3,2,1,0:T(8,128)S(1)}, u32[]{:S(2)}, u32[]{:S(2)}) async-start(f32[32,4,2,8,128]{4,3,2,1,0:T(8,128)} %whiten.3), calls=%async_computation | async-start | bytes 2097152 | tf_op jit(solution)/shard_map/all_to_all | solution.py:376
  13.0 10.8 %whiten.2 = (f32[2,12,2,8,128]{4,3,2,1,0:T(8,128)}, f32[2,12,2,8,128]{4,3,2,1,0:T(8,128)}, f32[2,12,2,8,128]{4,3,2,1,0:T(8,128)}, f32[2,12,2,8,128]{4,3,2,1,0:T(...) custom-call(s32[1]{0:T(128)} %bitcast.me_ref, ...), custom_call_target="tpu_custom_call" | custom-call | tf_op jit(solution)/shard_map/whiten/pallas_call | solution.py:139
  30.4 2.7 %collective-permute-done.refs_1_.refs_2_ = f32[2,192,128]{2,1,0:T(8,128)S(1)} collective-permute-done((f32[2,192,128]{2,1,0:T(8,128)}, f32[2,192,128]{2,1,0:T(8,128)S(1)}, u32[]{:S(2)}, u32[]{:S(2)}) %collective-permute-start) | collective-permute-done | bytes 196640 | tf_op jit(solution)/shard_map/ppermute | solution.py:331
  33.1 2.9 %collective-permute-start.5 = (f32[2,192,128]{2,1,0:T(8,128)}, f32[2,192,128]{2,1,0:T(8,128)S(1)}, u32[]{:S(2)}, u32[]{:S(2)}) collective-permute-start(f32[2,192,128]{2,1,0:T(8,128)} %bitcast.35), channel_id=1, source_target_pairs={{0,12},{1,13},{2,14},{3,15},{4,8},{5,9},{6,10},{7,11},{8,4},{9,5},... | collective-permute-start | bytes 589832 | tf_op jit(solution)/shard_map/ppermute | solution.py:331
  36.0 2.9 %collective-permute-done.1.refs_2_.refs_3_ = f32[2,192,128]{2,1,0:T(8,128)S(1)} collective-permute-done((f32[2,192,128]{2,1,0:T(8,128)}, f32[2,192,128]{2,1,0:T(8,128)S(1)}, u32[]{:S(2)}, u32[]{:S(2)}) %collective-permute-start.1) | collective-permute-done | bytes 196640 | tf_op jit(solution)/shard_map/ppermute | solution.py:331
  40.0 4.5 %collective-permute-done.4.refs_5_.refs_1_ = f32[2,192,128]{2,1,0:T(8,128)S(1)} collective-permute-done((f32[2,192,128]{2,1,0:T(8,128)}, f32[2,192,128]{2,1,0:T(8,128)S(1)}, u32[]{:S(2)}, u32[]{:S(2)}) %collective-permute-start.4) | collective-permute-done | bytes 196640 | tf_op jit(solution)/shard_map/ppermute | solution.py:331
  44.5 4.0 %collective-permute-done.5.refs_6_.refs_2_ = f32[2,192,128]{2,1,0:T(8,128)S(1)} collective-permute-done((f32[2,192,128]{2,1,0:T(8,128)}, f32[2,192,128]{2,1,0:T(8,128)S(1)}, u32[]{:S(2)}, u32[]{:S(2)}) %collective-permute-start.5) | collective-permute-done | bytes 196640 | tf_op jit(solution)/shard_map/ppermute | solution.py:331
  48.5 4.6 %collective-permute-done.6.refs_7_.refs_3_ = f32[2,192,128]{2,1,0:T(8,128)S(1)} collective-permute-done((f32[2,192,128]{2,1,0:T(8,128)}, f32[2,192,128]{2,1,0:T(8,128)S(1)}, u32[]{:S(2)}, u32[]{:S(2)}) %collective-permute-start.6) | collective-permute-done | bytes 196640 | tf_op jit(solution)/shard_map/ppermute | solution.py:331
  53.8 2.2 %bundle.1 = f32[1536,128]{1,0:T(8,128)} custom-call(s32[1]{0:T(128)} %bitcast.me_ref, f32[2,192,128]{2,1,0:T(8,128)} %bitcast.30, f32[2,192,128]{2,1,0:T(8,128)} %copy-done.4, f32[2,192,128]{2,1,0:T(8,128)} %copy-done.5, f32[2,192,128]{2,1,0:T(8,128)} %copy-done.6, f32[2,192,128]{2,1,0:T(8,128)} %copy-done.7, f32[2,192,128]{2,1,0:T(8,128)} %copy-done.1, ...), custom_call_target="tpu_custom_call" | custom-call | tf_op jit(solution)/shard_map/bundle/pallas_call | solution.py:197
  56.0 1.9 %collective-permute-start.18 = (f32[2,16,256]{2,1,0:T(8,128)S(1)}, f32[2,16,256]{2,1,0:T(8,128)S(1)}, u32[]{:S(2)}, u32[]{:S(2)}) collective-permute-start(f32[2,16,256]{2,1,0:T(8,128)S(1)} %copy-done.23), channel_id=1, source_target_pairs={{0,16},{1,17},{2,18},{3,19},{4,20},{5,21},{6,22},{7,23},{8,24},{9,... | collective-permute-start | bytes 98312 | tf_op jit(solution)/shard_map/ppermute | solution.py:331
  58.6 2.8 %collective-permute-done.18 = f32[2,16,256]{2,1,0:T(8,128)S(1)} collective-permute-done((f32[2,16,256]{2,1,0:T(8,128)S(1)}, f32[2,16,256]{2,1,0:T(8,128)S(1)}, u32[]{:S(2)}, u32[]{:S(2)}) %collective-permute-start.18) | collective-permute-done | bytes 32800 | tf_op jit(solution)/shard_map/ppermute | solution.py:331
  62.0 2.4 %collective-permute-start.24 = (f32[16,256]{1,0:T(8,128)S(1)}, f32[16,256]{1,0:T(8,128)S(1)}, u32[]{:S(2)}, u32[]{:S(2)}) collective-permute-start(f32[16,256]{1,0:T(8,128)S(1)} %fusion.refs_0_.refs_5_), channel_id=1, source_target_pairs={{0,12},{1,13},{2,14},{3,15},{4,8},{5,9},{6,10},{7,11},{8,4},{9,5},... | collective-permute-start | bytes 49160 | tf_op jit(solution)/shard_map/ppermute | solution.py:331
  65.3 2.9 %collective-permute-done.25.refs_7_.refs_12_ = f32[16,256]{1,0:T(8,128)S(1)} collective-permute-done((f32[16,256]{1,0:T(8,128)S(1)}, f32[16,256]{1,0:T(8,128)S(1)}, u32[]{:S(2)}, u32[]{:S(2)}) %collective-permute-start.25) | collective-permute-done | bytes 16416 | tf_op jit(solution)/shard_map/ppermute | solution.py:331
  69.0 3.0 %collective-permute-done.22.refs_4_.refs_9_ = f32[16,256]{1,0:T(8,128)S(1)} collective-permute-done((f32[16,256]{1,0:T(8,128)S(1)}, f32[16,256]{1,0:T(8,128)S(1)}, u32[]{:S(2)}, u32[]{:S(2)}) %collective-permute-start.22) | collective-permute-done | bytes 16416 | tf_op jit(solution)/shard_map/ppermute | solution.py:331
  73.7 2.1 %collective-permute-done.20.refs_2_.refs_7_ = f32[16,256]{1,0:T(8,128)S(1)} collective-permute-done((f32[16,256]{1,0:T(8,128)S(1)}, f32[16,256]{1,0:T(8,128)S(1)}, u32[]{:S(2)}, u32[]{:S(2)}) %collective-permute-start.20) | collective-permute-done | bytes 16416 | tf_op jit(solution)/shard_map/ppermute | solution.py:331
  75.9 2.5 %collective-permute-start.10 = (f32[192,128]{1,0:T(8,128)}, f32[192,128]{1,0:T(8,128)S(1)}, u32[]{:S(2)}, u32[]{:S(2)}) collective-permute-start(f32[192,128]{1,0:T(8,128)} %bitcast.54), channel_id=1, source_target_pairs={{0,24},{1,25},{2,26},{3,27},{4,28},{5,29},{6,30},{7,31},{8,16},{9,... | collective-permute-start | bytes 294920 | tf_op jit(solution)/shard_map/ppermute | solution.py:331
  79.1 3.1 %collective-permute-start.12 = (f32[192,128]{1,0:T(8,128)}, f32[192,128]{1,0:T(8,128)S(1)}, u32[]{:S(2)}, u32[]{:S(2)}) collective-permute-start(f32[192,128]{1,0:T(8,128)} %bitcast.52), channel_id=1, source_target_pairs={{0,26},{1,27},{2,24},{3,25},{4,30},{5,31},{6,28},{7,29},{8,18},{9,... | collective-permute-start | bytes 294920 | tf_op jit(solution)/shard_map/ppermute | solution.py:331
  82.2 1.7 %collective-permute-start.13 = (f32[192,128]{1,0:T(8,128)}, f32[192,128]{1,0:T(8,128)S(1)}, u32[]{:S(2)}, u32[]{:S(2)}) collective-permute-start(f32[192,128]{1,0:T(8,128)} %bitcast.51), channel_id=1, source_target_pairs={{0,27},{1,26},{2,25},{3,24},{4,31},{5,30},{6,29},{7,28},{8,19},{9,... | collective-permute-start | bytes 294920 | tf_op jit(solution)/shard_map/ppermute | solution.py:331
  85.6 8.7 %collective-permute-start.28 = (f32[192,128]{1,0:T(8,128)}, f32[192,128]{1,0:T(8,128)S(1)}, u32[]{:S(2)}, u32[]{:S(2)}) collective-permute-start(f32[192,128]{1,0:T(8,128)} %bitcast.49), channel_id=1, source_target_pairs={{0,17},{1,16},{2,19},{3,18},{4,21},{5,20},{6,23},{7,22},{8,25},{9,... | collective-permute-start | bytes 294920 | tf_op jit(solution)/shard_map/ppermute | solution.py:331
  94.2 3.6 %collective-permute-start.29 = (f32[192,128]{1,0:T(8,128)}, f32[192,128]{1,0:T(8,128)S(1)}, u32[]{:S(2)}, u32[]{:S(2)}) collective-permute-start(f32[192,128]{1,0:T(8,128)} %bitcast.48), channel_id=1, source_target_pairs={{0,18},{1,19},{2,16},{3,17},{4,22},{5,23},{6,20},{7,21},{8,26},{9,... | collective-permute-start | bytes 294920 | tf_op jit(solution)/shard_map/ppermute | solution.py:331
  99.4 4.8 %collective-permute-done.27.refs_6_ = f32[192,128]{1,0:T(8,128)S(1)} collective-permute-done((f32[192,128]{1,0:T(8,128)}, f32[192,128]{1,0:T(8,128)S(1)}, u32[]{:S(2)}, u32[]{:S(2)}) %collective-permute-start.27) | collective-permute-done | bytes 98336 | tf_op jit(solution)/shard_map/ppermute | solution.py:331
  104.2 1.7 %collective-permute-done.28.refs_7_ = f32[192,128]{1,0:T(8,128)S(1)} collective-permute-done((f32[192,128]{1,0:T(8,128)}, f32[192,128]{1,0:T(8,128)S(1)}, u32[]{:S(2)}, u32[]{:S(2)}) %collective-permute-start.28) | collective-permute-done | bytes 98336 | tf_op jit(solution)/shard_map/ppermute | solution.py:331
  106.5 3.8 %collective-permute-done.29.refs_8_ = f32[192,128]{1,0:T(8,128)S(1)} collective-permute-done((f32[192,128]{1,0:T(8,128)}, f32[192,128]{1,0:T(8,128)S(1)}, u32[]{:S(2)}, u32[]{:S(2)}) %collective-permute-start.29) | collective-permute-done | bytes 98336 | tf_op jit(solution)/shard_map/ppermute | solution.py:331
  110.3 5.1 %collective-permute-done.30.refs_9_ = f32[192,128]{1,0:T(8,128)S(1)} collective-permute-done((f32[192,128]{1,0:T(8,128)}, f32[192,128]{1,0:T(8,128)S(1)}, u32[]{:S(2)}, u32[]{:S(2)}) %collective-permute-start.30) | collective-permute-done | bytes 98336 | tf_op jit(solution)/shard_map/ppermute | solution.py:331
  115.4 3.4 %collective-permute-start.14 = (f32[192,128]{1,0:T(8,128)}, f32[192,128]{1,0:T(8,128)S(1)}, u32[]{:S(2)}, u32[]{:S(2)}) collective-permute-start(f32[192,128]{1,0:T(8,128)} %bitcast.44), channel_id=1, source_target_pairs={{0,28},{1,29},{2,30},{3,31},{4,24},{5,25},{6,26},{7,27},{8,20},{9,... | collective-permute-start | bytes 294920 | tf_op jit(solution)/shard_map/ppermute | solution.py:331
  118.9 2.1 %collective-permute-start.15 = (f32[192,128]{1,0:T(8,128)}, f32[192,128]{1,0:T(8,128)S(1)}, u32[]{:S(2)}, u32[]{:S(2)}) collective-permute-start(f32[192,128]{1,0:T(8,128)} %bitcast.43), channel_id=1, source_target_pairs={{0,29},{1,28},{2,31},{3,30},{4,25},{5,24},{6,27},{7,26},{8,21},{9,... | collective-permute-start | bytes 294920 | tf_op jit(solution)/shard_map/ppermute | solution.py:331
  121.0 2.7 %collective-permute-start.16 = (f32[192,128]{1,0:T(8,128)}, f32[192,128]{1,0:T(8,128)S(1)}, u32[]{:S(2)}, u32[]{:S(2)}) collective-permute-start(f32[192,128]{1,0:T(8,128)} %bitcast.42), channel_id=1, source_target_pairs={{0,30},{1,31},{2,28},{3,29},{4,26},{5,27},{6,24},{7,25},{8,22},{9,... | collective-permute-start | bytes 294920 | tf_op jit(solution)/shard_map/ppermute | solution.py:331
  123.6 3.3 %collective-permute-start.17 = (f32[192,128]{1,0:T(8,128)}, f32[192,128]{1,0:T(8,128)S(1)}, u32[]{:S(2)}, u32[]{:S(2)}) collective-permute-start(f32[192,128]{1,0:T(8,128)} %bitcast.41), channel_id=1, source_target_pairs={{0,31},{1,30},{2,29},{3,28},{4,27},{5,26},{6,25},{7,24},{8,23},{9,... | collective-permute-start | bytes 294920 | tf_op jit(solution)/shard_map/ppermute | solution.py:331
  127.6 3.9 %mix.1 = (bf16[512,260]{1,0:T(8,128)(2,1)}, bf16[512,260]{1,0:T(8,128)(2,1)}, bf16[512,252]{1,0:T(8,128)(2,1)}, bf16[512,252]{1,0:T(8,128)(2,1)}) custom-call(s32[1]{0:T(128)} %bitcast.me_ref, s32[1,260]{1,0:T(1,128)} %constant.38.clone.refs_0_, s32[1,260]{1,0:T(1,128)} %constant.39.clone.refs_1_, s32[1,252]{1,0:T(1,128)} %constant.40.clone.refs_2_, ...), custom_call_target="tpu_custom_call" | custom-call | tf_op jit(solution)/shard_map/mix/pallas_call | solution.py:248
  132.5 7.1 %solve.2.refs_16_ = f32[512,2048]{1,0:T(8,128)} custom-call(s32[1]{0:T(128)} %bitcast.me_ref, f32[2048,128]{1,0:T(8,128)} %bitcast.29, f32[2,192,128]{2,1,0:T(8,128)} %bitcast.31, f32[2,192,128]{2,1,0:T(8,128)} %copy-done.4, f32[2,192,128]{2,1,0:T(8,128)} %copy-done.5, f32[2,192,128]{2,1,0:T(8,128)} %copy-done.6, f32[2,192,128]{2,1,0:T(8,128)} %copy-done.7, ...), custom_call_target="tpu_custom_call" | custom-call | tf_op jit(solution)/shard_map/solve/pallas_call | solution.py:287
  139.7 5.5 %solve.3 = f32[512,2048]{1,0:T(8,128)} custom-call(s32[1]{0:T(128)} %bitcast.me_ref, f32[1536,128]{1,0:T(8,128)S(1)} %collective-permute-done.7.refs_0_, f32[2,192,128]{2,1,0:T(8,128)} %copy-done.1, f32[2,192,128]{2,1,0:T(8,128)} %copy-done.2, f32[2,192,128]{2,1,0:T(8,128)} %copy-done.3, ...), custom_call_target="tpu_custom_call", output_to_operand_aliasing={{}: (17, {})} | custom-call | tf_op jit(solution)/shard_map/solve/pallas_call | solution.py:287
  (93 shorter events, 19.2 us)
Async XLA Ops:
  5.5 126.0 %all-to-all-start = ((f32[32,4,2,8,128]{4,3,2,1,0:T(8,128)}), f32[32,4,2,8,128]{4,3,2,1,0:T(8,128)S(1)}, u32[]{:S(2)}, u32[]{:S(2)}) async-start(f32[32,4,2,8,128]{4,3,2,1,0:T(8,128)} %whiten.3), calls=%async_computation | async-start | bytes 2097152 | tf_op jit(solution)/shard_map/all_to_all | solution.py:376
  23.8 9.3 %collective-permute-start = (f32[2,192,128]{2,1,0:T(8,128)}, f32[2,192,128]{2,1,0:T(8,128)S(1)}, u32[]{:S(2)}, u32[]{:S(2)}) collective-permute-start(f32[2,192,128]{2,1,0:T(8,128)} %bitcast.40), channel_id=1, source_target_pairs={{0,2},{1,3},{2,0},{3,1},{4,6},{5,7},{6,4},{7,5},{8,10},{9,11},{10,... | collective-permute-start | bytes 589832 | tf_op jit(solution)/shard_map/ppermute | solution.py:331
  25.5 13.5 %collective-permute-start.1 = (f32[2,192,128]{2,1,0:T(8,128)}, f32[2,192,128]{2,1,0:T(8,128)S(1)}, u32[]{:S(2)}, u32[]{:S(2)}) collective-permute-start(f32[2,192,128]{2,1,0:T(8,128)} %bitcast.39), channel_id=1, source_target_pairs={{0,4},{1,5},{2,6},{3,7},{4,0},{5,1},{6,2},{7,3},{8,12},{9,13},{10,... | collective-permute-start | bytes 589832 | tf_op jit(solution)/shard_map/ppermute | solution.py:331
  26.9 13.1 %collective-permute-start.2 = (f32[2,192,128]{2,1,0:T(8,128)}, f32[2,192,128]{2,1,0:T(8,128)S(1)}, u32[]{:S(2)}, u32[]{:S(2)}) collective-permute-start(f32[2,192,128]{2,1,0:T(8,128)} %bitcast.38), channel_id=1, source_target_pairs={{0,6},{1,7},{2,4},{3,5},{4,2},{5,3},{6,0},{7,1},{8,14},{9,15},{10,... | collective-permute-start | bytes 589832 | tf_op jit(solution)/shard_map/ppermute | solution.py:331
  27.4 12.6 %collective-permute-start.3 = (f32[2,192,128]{2,1,0:T(8,128)}, f32[2,192,128]{2,1,0:T(8,128)S(1)}, u32[]{:S(2)}, u32[]{:S(2)}) collective-permute-start(f32[2,192,128]{2,1,0:T(8,128)} %bitcast.37), channel_id=1, source_target_pairs={{0,8},{1,9},{2,10},{3,11},{4,12},{5,13},{6,14},{7,15},{8,0},{9,1},... | collective-permute-start | bytes 589832 | tf_op jit(solution)/shard_map/ppermute | solution.py:331
  29.0 15.5 %collective-permute-start.4 = (f32[2,192,128]{2,1,0:T(8,128)}, f32[2,192,128]{2,1,0:T(8,128)S(1)}, u32[]{:S(2)}, u32[]{:S(2)}) collective-permute-start(f32[2,192,128]{2,1,0:T(8,128)} %bitcast.36), channel_id=1, source_target_pairs={{0,10},{1,11},{2,8},{3,9},{4,14},{5,15},{6,12},{7,13},{8,2},{9,3},... | collective-permute-start | bytes 589832 | tf_op jit(solution)/shard_map/ppermute | solution.py:331
  33.1 15.4 %collective-permute-start.5 = (f32[2,192,128]{2,1,0:T(8,128)}, f32[2,192,128]{2,1,0:T(8,128)S(1)}, u32[]{:S(2)}, u32[]{:S(2)}) collective-permute-start(f32[2,192,128]{2,1,0:T(8,128)} %bitcast.35), channel_id=1, source_target_pairs={{0,12},{1,13},{2,14},{3,15},{4,8},{5,9},{6,10},{7,11},{8,4},{9,5},... | collective-permute-start | bytes 589832 | tf_op jit(solution)/shard_map/ppermute | solution.py:331
  38.9 14.2 %collective-permute-start.6 = (f32[2,192,128]{2,1,0:T(8,128)}, f32[2,192,128]{2,1,0:T(8,128)S(1)}, u32[]{:S(2)}, u32[]{:S(2)}) collective-permute-start(f32[2,192,128]{2,1,0:T(8,128)} %bitcast.34), channel_id=1, source_target_pairs={{0,14},{1,15},{2,12},{3,13},{4,10},{5,11},{6,8},{7,9},{8,6},{9,7},... | collective-permute-start | bytes 589832 | tf_op jit(solution)/shard_map/ppermute | solution.py:331
  56.0 83.7 %collective-permute-start.7 = (f32[1536,128]{1,0:T(8,128)}, f32[1536,128]{1,0:T(8,128)S(1)}, u32[]{:S(2)}, u32[]{:S(2)}) collective-permute-start(f32[1536,128]{1,0:T(8,128)} %bundle.1), channel_id=1, source_target_pairs={{0,1},{1,0},{2,3},{3,2},{4,5},{5,4},{6,7},{7,6},{8,9},{9,8},{10,11... | collective-permute-start | bytes 2359304 | tf_op jit(solution)/shard_map/ppermute | solution.py:331
  56.0 5.4 %collective-permute-start.18 = (f32[2,16,256]{2,1,0:T(8,128)S(1)}, f32[2,16,256]{2,1,0:T(8,128)S(1)}, u32[]{:S(2)}, u32[]{:S(2)}) collective-permute-start(f32[2,16,256]{2,1,0:T(8,128)S(1)} %copy-done.23), channel_id=1, source_target_pairs={{0,16},{1,17},{2,18},{3,19},{4,20},{5,21},{6,22},{7,23},{8,24},{9,... | collective-permute-start | bytes 98312 | tf_op jit(solution)/shard_map/ppermute | solution.py:331
  57.9 21.2 %collective-permute-start.8 = (f32[192,128]{1,0:T(8,128)}, f32[192,128]{1,0:T(8,128)S(1)}, u32[]{:S(2)}, u32[]{:S(2)}) collective-permute-start(f32[192,128]{1,0:T(8,128)} %bitcast.56), channel_id=1, source_target_pairs={{0,22},{1,23},{2,20},{3,21},{4,18},{5,19},{6,16},{7,17},{8,30},{9,... | collective-permute-start | bytes 294920 | tf_op jit(solution)/shard_map/ppermute | solution.py:331
  61.4 6.9 %collective-permute-start.25 = (f32[16,256]{1,0:T(8,128)S(1)}, f32[16,256]{1,0:T(8,128)S(1)}, u32[]{:S(2)}, u32[]{:S(2)}) collective-permute-start(f32[16,256]{1,0:T(8,128)S(1)} %fusion.refs_0_.refs_5_), channel_id=1, source_target_pairs={{0,14},{1,15},{2,12},{3,13},{4,10},{5,11},{6,8},{7,9},{8,6},{9,7},... | collective-permute-start | bytes 49160 | tf_op jit(solution)/shard_map/ppermute | solution.py:331
  62.0 6.3 %collective-permute-start.24 = (f32[16,256]{1,0:T(8,128)S(1)}, f32[16,256]{1,0:T(8,128)S(1)}, u32[]{:S(2)}, u32[]{:S(2)}) collective-permute-start(f32[16,256]{1,0:T(8,128)S(1)} %fusion.refs_0_.refs_5_), channel_id=1, source_target_pairs={{0,12},{1,13},{2,14},{3,15},{4,8},{5,9},{6,10},{7,11},{8,4},{9,5},... | collective-permute-start | bytes 49160 | tf_op jit(solution)/shard_map/ppermute | solution.py:331
  64.3 4.6 %collective-permute-start.23 = (f32[16,256]{1,0:T(8,128)S(1)}, f32[16,256]{1,0:T(8,128)S(1)}, u32[]{:S(2)}, u32[]{:S(2)}) collective-permute-start(f32[16,256]{1,0:T(8,128)S(1)} %fusion.refs_0_.refs_5_), channel_id=1, source_target_pairs={{0,10},{1,11},{2,8},{3,9},{4,14},{5,15},{6,12},{7,13},{8,2},{9,3},... | collective-permute-start | bytes 49160 | tf_op jit(solution)/shard_map/ppermute | solution.py:331
  68.3 4.7 %collective-permute-start.21 = (f32[16,256]{1,0:T(8,128)S(1)}, f32[16,256]{1,0:T(8,128)S(1)}, u32[]{:S(2)}, u32[]{:S(2)}) collective-permute-start(f32[16,256]{1,0:T(8,128)S(1)} %fusion.refs_0_.refs_5_), channel_id=1, source_target_pairs={{0,6},{1,7},{2,4},{3,5},{4,2},{5,3},{6,0},{7,1},{8,14},{9,15},{10,... | collective-permute-start | bytes 49160 | tf_op jit(solution)/shard_map/ppermute | solution.py:331
  68.9 13.2 %collective-permute-start.9 = (f32[192,128]{1,0:T(8,128)}, f32[192,128]{1,0:T(8,128)S(1)}, u32[]{:S(2)}, u32[]{:S(2)}) collective-permute-start(f32[192,128]{1,0:T(8,128)} %bitcast.55), channel_id=1, source_target_pairs={{0,23},{1,22},{2,21},{3,20},{4,19},{5,18},{6,17},{7,16},{8,31},{9,... | collective-permute-start | bytes 294920 | tf_op jit(solution)/shard_map/ppermute | solution.py:331
  73.0 5.4 %collective-permute-start.19 = (f32[16,256]{1,0:T(8,128)S(1)}, f32[16,256]{1,0:T(8,128)S(1)}, u32[]{:S(2)}, u32[]{:S(2)}) collective-permute-start(f32[16,256]{1,0:T(8,128)S(1)} %fusion.refs_0_.refs_5_), channel_id=1, source_target_pairs={{0,2},{1,3},{2,0},{3,1},{4,6},{5,7},{6,4},{7,5},{8,10},{9,11},{10,... | collective-permute-start | bytes 49160 | tf_op jit(solution)/shard_map/ppermute | solution.py:331
  75.9 8.0 %collective-permute-start.10 = (f32[192,128]{1,0:T(8,128)}, f32[192,128]{1,0:T(8,128)S(1)}, u32[]{:S(2)}, u32[]{:S(2)}) collective-permute-start(f32[192,128]{1,0:T(8,128)} %bitcast.54), channel_id=1, source_target_pairs={{0,24},{1,25},{2,26},{3,27},{4,28},{5,29},{6,30},{7,31},{8,16},{9,... | collective-permute-start | bytes 294920 | tf_op jit(solution)/shard_map/ppermute | solution.py:331
  78.4 7.2 %collective-permute-start.11 = (f32[192,128]{1,0:T(8,128)}, f32[192,128]{1,0:T(8,128)S(1)}, u32[]{:S(2)}, u32[]{:S(2)}) collective-permute-start(f32[192,128]{1,0:T(8,128)} %bitcast.53), channel_id=1, source_target_pairs={{0,25},{1,24},{2,27},{3,26},{4,29},{5,28},{6,31},{7,30},{8,17},{9,... | collective-permute-start | bytes 294920 | tf_op jit(solution)/shard_map/ppermute | solution.py:331
  79.1 15.1 %collective-permute-start.12 = (f32[192,128]{1,0:T(8,128)}, f32[192,128]{1,0:T(8,128)S(1)}, u32[]{:S(2)}, u32[]{:S(2)}) collective-permute-start(f32[192,128]{1,0:T(8,128)} %bitcast.52), channel_id=1, source_target_pairs={{0,26},{1,27},{2,24},{3,25},{4,30},{5,31},{6,28},{7,29},{8,18},{9,... | collective-permute-start | bytes 294920 | tf_op jit(solution)/shard_map/ppermute | solution.py:331
  82.2 17.2 %collective-permute-start.13 = (f32[192,128]{1,0:T(8,128)}, f32[192,128]{1,0:T(8,128)S(1)}, u32[]{:S(2)}, u32[]{:S(2)}) collective-permute-start(f32[192,128]{1,0:T(8,128)} %bitcast.51), channel_id=1, source_target_pairs={{0,27},{1,26},{2,25},{3,24},{4,31},{5,30},{6,29},{7,28},{8,19},{9,... | collective-permute-start | bytes 294920 | tf_op jit(solution)/shard_map/ppermute | solution.py:331
  83.9 20.3 %collective-permute-start.27 = (f32[192,128]{1,0:T(8,128)}, f32[192,128]{1,0:T(8,128)S(1)}, u32[]{:S(2)}, u32[]{:S(2)}) collective-permute-start(f32[192,128]{1,0:T(8,128)} %bitcast.50), channel_id=1, source_target_pairs={{0,16},{1,17},{2,18},{3,19},{4,20},{5,21},{6,22},{7,23},{8,24},{9,... | collective-permute-start | bytes 294920 | tf_op jit(solution)/shard_map/ppermute | solution.py:331
  85.6 20.4 %collective-permute-start.28 = (f32[192,128]{1,0:T(8,128)}, f32[192,128]{1,0:T(8,128)S(1)}, u32[]{:S(2)}, u32[]{:S(2)}) collective-permute-start(f32[192,128]{1,0:T(8,128)} %bitcast.49), channel_id=1, source_target_pairs={{0,17},{1,16},{2,19},{3,18},{4,21},{5,20},{6,23},{7,22},{8,25},{9,... | collective-permute-start | bytes 294920 | tf_op jit(solution)/shard_map/ppermute | solution.py:331
  94.2 16.1 %collective-permute-start.29 = (f32[192,128]{1,0:T(8,128)}, f32[192,128]{1,0:T(8,128)S(1)}, u32[]{:S(2)}, u32[]{:S(2)}) collective-permute-start(f32[192,128]{1,0:T(8,128)} %bitcast.48), channel_id=1, source_target_pairs={{0,18},{1,19},{2,16},{3,17},{4,22},{5,23},{6,20},{7,21},{8,26},{9,... | collective-permute-start | bytes 294920 | tf_op jit(solution)/shard_map/ppermute | solution.py:331
  99.4 24.3 %collective-permute-start.26 = (f32[128,256]{1,0:T(8,128)}, f32[128,256]{1,0:T(8,128)S(1)}, u32[]{:S(2)}, u32[]{:S(2)}) collective-permute-start(f32[128,256]{1,0:T(8,128)} %stack.1), channel_id=1, source_target_pairs={{0,1},{1,0},{2,3},{3,2},{4,5},{5,4},{6,7},{7,6},{8,9},{9,8},{10,11... | collective-permute-start | bytes 393224 | tf_op jit(solution)/shard_map/ppermute | solution.py:331
  104.2 11.2 %collective-permute-start.30 = (f32[192,128]{1,0:T(8,128)}, f32[192,128]{1,0:T(8,128)S(1)}, u32[]{:S(2)}, u32[]{:S(2)}) collective-permute-start(f32[192,128]{1,0:T(8,128)} %bitcast.47), channel_id=1, source_target_pairs={{0,19},{1,18},{2,17},{3,16},{4,23},{5,22},{6,21},{7,20},{8,27},{9,... | collective-permute-start | bytes 294920 | tf_op jit(solution)/shard_map/ppermute | solution.py:331
  105.9 12.9 %collective-permute-start.31 = (f32[192,128]{1,0:T(8,128)}, f32[192,128]{1,0:T(8,128)S(1)}, u32[]{:S(2)}, u32[]{:S(2)}) collective-permute-start(f32[192,128]{1,0:T(8,128)} %bitcast.46), channel_id=1, source_target_pairs={{0,20},{1,21},{2,22},{3,23},{4,16},{5,17},{6,18},{7,19},{8,28},{9,... | collective-permute-start | bytes 294920 | tf_op jit(solution)/shard_map/ppermute | solution.py:331
  110.3 10.7 %collective-permute-start.32 = (f32[192,128]{1,0:T(8,128)}, f32[192,128]{1,0:T(8,128)S(1)}, u32[]{:S(2)}, u32[]{:S(2)}) collective-permute-start(f32[192,128]{1,0:T(8,128)} %bitcast.45), channel_id=1, source_target_pairs={{0,21},{1,20},{2,23},{3,22},{4,17},{5,16},{6,19},{7,18},{8,29},{9,... | collective-permute-start | bytes 294920 | tf_op jit(solution)/shard_map/ppermute | solution.py:331
  115.4 24.2 %collective-permute-start.14 = (f32[192,128]{1,0:T(8,128)}, f32[192,128]{1,0:T(8,128)S(1)}, u32[]{:S(2)}, u32[]{:S(2)}) collective-permute-start(f32[192,128]{1,0:T(8,128)} %bitcast.44), channel_id=1, source_target_pairs={{0,28},{1,29},{2,30},{3,31},{4,24},{5,25},{6,26},{7,27},{8,20},{9,... | collective-permute-start | bytes 294920 | tf_op jit(solution)/shard_map/ppermute | solution.py:331
  118.9 20.8 %collective-permute-start.15 = (f32[192,128]{1,0:T(8,128)}, f32[192,128]{1,0:T(8,128)S(1)}, u32[]{:S(2)}, u32[]{:S(2)}) collective-permute-start(f32[192,128]{1,0:T(8,128)} %bitcast.43), channel_id=1, source_target_pairs={{0,29},{1,28},{2,31},{3,30},{4,25},{5,24},{6,27},{7,26},{8,21},{9,... | collective-permute-start | bytes 294920 | tf_op jit(solution)/shard_map/ppermute | solution.py:331
  121.0 18.7 %collective-permute-start.16 = (f32[192,128]{1,0:T(8,128)}, f32[192,128]{1,0:T(8,128)S(1)}, u32[]{:S(2)}, u32[]{:S(2)}) collective-permute-start(f32[192,128]{1,0:T(8,128)} %bitcast.42), channel_id=1, source_target_pairs={{0,30},{1,31},{2,28},{3,29},{4,26},{5,27},{6,24},{7,25},{8,22},{9,... | collective-permute-start | bytes 294920 | tf_op jit(solution)/shard_map/ppermute | solution.py:331
  123.6 16.0 %collective-permute-start.17 = (f32[192,128]{1,0:T(8,128)}, f32[192,128]{1,0:T(8,128)S(1)}, u32[]{:S(2)}, u32[]{:S(2)}) collective-permute-start(f32[192,128]{1,0:T(8,128)} %bitcast.41), channel_id=1, source_target_pairs={{0,31},{1,30},{2,29},{3,28},{4,27},{5,26},{6,25},{7,24},{8,23},{9,... | collective-permute-start | bytes 294920 | tf_op jit(solution)/shard_map/ppermute | solution.py:331
  (26 other events, 460.0 us)
